TPU v7x, 512 devices: a whole 4x8x8 slice. The times are simulated.
512 devices in a mesh: grp: 16 (over y, core), col: 32 (over x, z).
Axes of the slice: x: 4, y: 8, z: 8, core: 2. Of those that a mesh axis runs over, the one named last changes fastest.
Arguments:
- conc: float32 [12, 256, 65536], P(None, 'col', 'grp'), may hold values from 0.1 to 10
- porosity: float32 [256, 65536], P('col', 'grp'), may hold values from 0.2 to 0.5
- cell_cond: float32 [256, 65536], P('col', 'grp'), may hold values from 0.5 to 2
- soil_class: int32 [65536], P(('grp', 'col')), may hold values from 0 to 15
- active: int32 [65536], P(('grp', 'col')), may hold values from 64 to 256
- class_cond: float32 [16], replicated, may hold values from 20 to 400
- sorb_affinity: float32 [16, 12], replicated, may hold values from 0.05 to 5
- sorb_capacity: float32 [16], replicated, may hold values from 1 to 20
- surf_conc: float32 [12, 262144], P(None, ('grp', 'col')), may hold values from 0.1 to 10
- surf_rate: float32 [262144], P(('grp', 'col')), may hold values from 0.1 to 2
- surf_group: int32 [262144, 1], P(('grp', 'col')), may hold values from 0 to 15; in each aligned block of 512 rows (0 to 511, 512 to 1023, ...) at most 128 rows name the same one
- surf_local: int32 [262144], P(('grp', 'col')), may hold values from 0 to 127
Outputs:
- log_free: float32 [12, 256, 65536], P(None, 'col', 'grp')
- surf_flux: float32 [12, 262144], P(None, ('grp', 'col'))
Inputs may be any that keep to these rules, and one draw needn't show every extreme that they name: `surf_group`: among the rows of one device (aligned blocks of 512 rows) at most 128 name the same group, a bound that some block reaches of one device.
All inputs are finite; a program needn't handle non-finite values.
Results may differ from a plain program's by a relative error of at most 0.0003.
Values sent between devices are 32-bit elements; how exact they have to be, the bound alone decides.
No kernel may reach another device: no remote copies, remote signals or barrier semaphores. Data moves between devices by JAX's collectives and lax.ppermute only.
A program may use at most 128 MiB of HBM per device.

v0:
```python
import functools
import jax
import jax.numpy as jnp
from jax import lax
from jax.experimental import pallas as pl
from jax.experimental.pallas import tpu as pltpu
from jax.sharding import PartitionSpec as P

ITERS = 4
LANES = 128
F32 = jnp.float32
INTERPRET = False


def split3(v):
    hi = v.astype(jnp.bfloat16)
    rest = v - hi.astype(F32)
    mid = rest.astype(jnp.bfloat16)
    lo = (rest - mid.astype(F32)).astype(jnp.bfloat16)
    return hi, mid, lo


def rows_iota(shape):
    return lax.broadcasted_iota(jnp.int32, shape, 0)


def surf_pack_kernel(conc_ref, rate_ref, group_ref, local_ref, send_ref, lhs_ref):
    comps, n = conc_ref.shape
    groups = send_ref.shape[0]
    rate = rate_ref[...]
    vals = jnp.concatenate(
        [conc_ref[...] * rate, rate, jnp.zeros((15 - comps, n), F32)], axis=0
    )
    hi, mid, lo = split3(vals)
    group = group_ref[...]
    for g in range(groups):
        keep = group == g
        for i, part in enumerate((hi, mid, lo)):
            lhs_ref[i, 16 * g : 16 * g + 16, :] = jnp.where(
                keep, part.astype(F32), 0.0
            ).astype(jnp.bfloat16)
    place = (rows_iota((LANES, n)) == local_ref[...]).astype(F32).astype(jnp.bfloat16)
    dims = (((1,), (1,)), ((), ()))
    total = sum(
        lax.dot_general(lhs_ref[i], place, dims, preferred_element_type=F32)
        for i in (2, 1, 0)
    )
    send_ref[...] = total.reshape(groups, 16, LANES)


def surf_flux_kernel(table_ref, conc_ref, rate_ref, group_ref, local_ref, flux_ref):
    comps, n = conc_ref.shape
    groups = table_ref.shape[0]
    table = table_ref[...].reshape(groups * 16, LANES)
    place = (rows_iota((LANES, n)) == local_ref[...]).astype(F32).astype(jnp.bfloat16)
    hi, mid, lo = split3(table)
    picked = jnp.dot(lo, place, preferred_element_type=F32)
    picked += jnp.dot(mid, place, preferred_element_type=F32)
    picked += jnp.dot(hi, place, preferred_element_type=F32)
    group = group_ref[...]
    top = jnp.zeros((16, n), F32)
    for g in range(groups):
        top = jnp.where(group == g, picked[16 * g : 16 * g + 16], top)
    rate = rate_ref[...]
    flux_ref[...] = rate * conc_ref[...] - rate * top[:comps]


def eliminate_kernel(
    first_ref, table_ref, conc_ref, theta_ref, cond_ref, meta_ref, send_ref, g_ref, vw_ref
):
    comps = conc_ref.shape[0]
    tiles = send_ref.shape[0]
    shape = (8, LANES)
    row = rows_iota(shape)
    zero = jnp.zeros(shape, F32)
    layer = first_ref[0] + row

    def roll(v, d):
        return pltpu.roll(v, d % 8, 0)

    for t in range(tiles):
        cols = pl.ds(t * LANES, LANES)
        classes = meta_ref[t, 0:1, :]
        active = meta_ref[t, 1:2, :]
        scale = jnp.zeros((1, LANES), F32)
        for k in range(table_ref.shape[0]):
            scale = jnp.where(classes == k, table_ref[k], scale)
        theta = theta_ref[:, cols]
        scaled = cond_ref[:, cols] * scale
        below = roll(scaled, -1)
        link = 2.0 * scaled * below / (scaled + below)
        link = jnp.where((row < 7) & (layer + 1 < active), link, zero)
        link_up = roll(link, 1)
        up = jnp.where((row >= 2) & (row <= 6), link_up, zero)
        dn = jnp.where((row >= 1) & (row <= 5), link, zero)
        r_v = jnp.where(row == 1, link_up, zero)
        r_w = jnp.where(row == 6, link, zero)
        r_e = jnp.where((row >= 1) & (row <= 6), theta, zero)
        excess = theta + r_v + r_w
        w1 = 1.0 / (excess + up + dn)
        t1 = excess * w1
        up1, dn1 = up, dn
        excess = excess + up * roll(t1, 1) + dn * roll(t1, -1)
        up2 = up * roll(up * w1, 1)
        dn2 = dn * roll(dn * w1, -1)
        w2 = 1.0 / (excess + up2 + dn2)
        t2 = excess * w2
        excess = excess + up2 * roll(t2, 2) + dn2 * roll(t2, -2)
        up3 = up2 * roll(up2 * w2, 2)
        dn3 = dn2 * roll(dn2 * w2, -2)
        far = up3 + dn3
        w3 = 1.0 / (excess + far)
        excess = excess + far * roll(excess * w3, 4)
        w4 = 1.0 / excess

        def solve(r):
            q = r * w1
            r = r + up1 * roll(q, 1) + dn1 * roll(q, -1)
            q = r * w2
            r = r + up2 * roll(q, 2) + dn2 * roll(q, -2)
            r = r + far * roll(r * w3, 4)
            return r * w4

        ends = jnp.where(row == 0, link, zero) + jnp.where(row == 7, link_up, zero)

        def onto_ends(own, inner):
            near = jnp.where(row == 0, roll(inner, -1), roll(inner, 1))
            return own + ends * near

        v = solve(r_v)
        w = solve(r_w)
        e = solve(r_e)
        vw_ref[0, :, cols] = jnp.where(row == 0, 1.0, v)
        vw_ref[1, :, cols] = jnp.where(row == 7, 1.0, w)
        diag = onto_ends(theta, e)
        cross = onto_ends(zero, w)
        mat = jnp.where(row == 0, diag, zero)
        mat = jnp.where(row == 1, roll(diag, 2), mat)
        mat = jnp.where(row == 2, roll(cross, 2), mat)
        mat = jnp.where(row == 3, roll(scaled, 3), mat)
        mat = jnp.where(row == 4, roll(scaled, 5), mat)
        send_ref[t, 24:32, :] = mat
        firsts, lasts, mixed = zero, zero, zero
        for j in range(comps):
            c = conc_ref[j, :, cols]
            g = solve(r_e * c)
            g_ref[j, :, cols] = g
            z = onto_ends(theta * c, g)
            if j < 8:
                z = roll(z, j) if j else z
                firsts = jnp.where(row == j, z, firsts)
                lasts = jnp.where(row == (j + 7) % 8, z, lasts)
            else:
                k = j - 8
                mixed = jnp.where(row == k, roll(z, k) if k else z, mixed)
                mixed = jnp.where(row == k + 4, roll(z, k + 5), mixed)
        send_ref[t, 0:8, :] = firsts
        send_ref[t, 8:16, :] = lasts
        send_ref[t, 16:24, :] = mixed


def first_row(j):
    return j if j < 8 else 16 + j - 8


def last_row(j):
    return 8 + (j + 7) % 8 if j < 8 else 20 + j - 8


def interface_kernel(recv_ref, surf_ref, active_ref, ends_ref, top_ref):
    blocks = ends_ref.shape[0] // 24
    comps = 12
    groups = top_ref.shape[0]
    shape = (blocks, LANES)
    row = rows_iota(shape)
    zero = jnp.zeros(shape, F32)

    def roll(v, d):
        return pltpu.roll(v, d % blocks, 0)

    def take(r):
        return recv_ref[pl.ds(r, blocks, stride=32), :]

    partial = surf_ref[0]
    for g in range(1, surf_ref.shape[0]):
        partial = partial + surf_ref[g]
    alpha = take(24) + jnp.where(row == 0, partial[comps : comps + 1], zero)
    beta, cross, s_first, s_last = take(25), take(26), take(27), take(28)
    s_above = roll(s_last, 1)
    link = 2.0 * s_above * s_first / (s_above + s_first)
    link = jnp.where((row > 0) & (8 * row < active_ref[...]), link, zero)
    wf = 1.0 / (alpha + cross + link)
    cross_w = cross * wf
    link_w = link * wf
    up = link * cross_w
    dn = roll(up, -1)
    excess = beta + alpha * cross_w + roll(alpha * link_w, -1)
    steps = []
    d = 1
    while d < blocks:
        w = 1.0 / (excess + up + dn)
        steps.append((d, up, dn, w))
        q = excess * w
        excess = excess + up * roll(q, d) + dn * roll(q, -d)
        up, dn = up * roll(up * w, d), dn * roll(dn * w, -d)
        d *= 2
    w_end = 1.0 / excess
    tops = []
    for j in range(comps):
        b = take(first_row(j)) + jnp.where(row == 0, partial[j : j + 1], zero)
        r = take(last_row(j)) + cross_w * b + roll(link_w * b, -1)
        for d, up, dn, w in steps:
            q = r * w
            r = r + up * roll(q, d) + dn * roll(q, -d)
        last = r * w_end
        first = link_w * roll(last, 1) + cross_w * last + wf * b
        ends_ref[pl.ds(j, blocks, stride=24), :] = first
        ends_ref[pl.ds(12 + j, blocks, stride=24), :] = last
        tops.append(first[0:1])
    top = jnp.concatenate(tops + [jnp.zeros((16 - comps, LANES), F32)], axis=0)
    for g in range(groups):
        top_ref[g] = top


def lookup_kernel(table_ref, meta_ref, out_ref):
    table = table_ref[...]
    classes = table.shape[1]
    hi, mid, lo = split3(table)
    for t in range(out_ref.shape[0]):
        hit = (rows_iota((classes, LANES)) == meta_ref[t, 0:1, :]).astype(F32)
        hit = hit.astype(jnp.bfloat16)
        out_ref[t] = (
            jnp.dot(lo, hit, preferred_element_type=F32)
            + jnp.dot(mid, hit, preferred_element_type=F32)
            + jnp.dot(hi, hit, preferred_element_type=F32)
        )


def speciate_kernel(g_ref, vw_ref, theta_ref, ends_ref, sorb_ref, out_ref):
    comps = g_ref.shape[0]
    tiles = ends_ref.shape[0]

    def tile(t, carry):
        cols = pl.ds(pl.multiple_of(t * LANES, LANES), LANES)
        theta = theta_ref[:, cols]
        v = vw_ref[0, :, cols]
        w = vw_ref[1, :, cols]
        cap = sorb_ref[t, comps : comps + 1, :]
        aff = [sorb_ref[t, j : j + 1, :] for j in range(comps)]
        sorb = [cap * a for a in aff]
        x, c, p, at = [], [], [], []
        for j in range(comps):
            total = (
                g_ref[j, :, cols]
                + v * ends_ref[t, j : j + 1, :]
                + w * ends_ref[t, 12 + j : 13 + j, :]
            )
            whole = theta + sorb[j]
            start = total / whole
            x.append(jnp.log(start))
            c.append(start)
            p.append(whole)
            at.append(aff[j] * total)
        for step in range(ITERS):
            ac = [aff[j] * c[j] for j in range(comps)]
            load = sum(ac[1:], ac[0])
            crowd = 1.0 + load
            hold = theta * crowd
            q = [1.0 / (hold + sorb[j]) for j in range(comps)]
            sq = [sorb[j] * q[j] for j in range(comps)]
            atq = [at[j] * q[j] for j in range(comps)]
            acq = [ac[j] * sq[j] for j in range(comps)]
            numer = load - crowd * sum(atq[1:], atq[0])
            lean = sum(acq[1:], acq[0])
            gain = 1.0 + numer / (crowd - lean)
            for j in range(comps):
                move = (theta - p[j]) * crowd * q[j] + sq[j] * gain
                move = jnp.clip(move, -1.0, 1.0)
                x[j] = x[j] - move
                if step < ITERS - 1:
                    c[j] = c[j] * jnp.exp(-move)
                    p[j] = p[j] * jnp.exp(move)
        for j in range(comps):
            out_ref[j, :, cols] = x[j]
        return carry

    lax.fori_loop(0, tiles, tile, 0)


VMEM = pltpu.VMEM


def full(memory_space=VMEM):
    return pl.BlockSpec(memory_space=memory_space)


def call(kernel, out_shape, n_in, **kw):
    n_out = len(out_shape) if isinstance(out_shape, (tuple, list)) else None
    out_specs = full() if n_out is None else tuple(full() for _ in range(n_out))
    return pl.pallas_call(
        kernel,
        out_shape=out_shape,
        in_specs=[full()] * n_in,
        out_specs=out_specs,
        interpret=INTERPRET,
        **kw,
    )


def body(
    conc,
    porosity,
    cell_cond,
    soil_class,
    active,
    class_cond,
    sorb_affinity,
    sorb_capacity,
    surf_conc,
    surf_rate,
    surf_group,
    surf_local,
):
    groups = lax.axis_size("grp")
    owners = lax.axis_size("col")
    comps, depth, width = conc.shape
    n = surf_conc.shape[1]
    sds = jax.ShapeDtypeStruct
    first = (lax.axis_index("col") * depth).astype(jnp.int32).reshape(1)

    meta = jnp.stack([soil_class, active])
    meta = jnp.broadcast_to(meta[None], (owners, 2, LANES))
    meta = lax.all_to_all(meta, "col", split_axis=0, concat_axis=0, tiled=True)

    rate = surf_rate.reshape(1, n)
    group = surf_group.reshape(1, n)
    local = surf_local.reshape(1, n)
    surf_send = call(
        surf_pack_kernel,
        sds((groups, 16, LANES), F32),
        4,
        scratch_shapes=[pltpu.VMEM((3, 16 * groups, n), jnp.bfloat16)],
        name="surf_pack",
    )(surf_conc, rate, group, local)
    surf_recv = lax.all_to_all(surf_send, "grp", split_axis=0, concat_axis=0, tiled=True)

    tiles = 4
    steps = owners // tiles
    wide = tiles * LANES
    send, g, vw = pl.pallas_call(
        eliminate_kernel,
        grid=(steps,),
        out_shape=(
            sds((owners, 32, LANES), F32),
            sds((comps, depth, width), F32),
            sds((2, depth, width), F32),
        ),
        in_specs=[
            pl.BlockSpec(memory_space=pltpu.SMEM),
            pl.BlockSpec(memory_space=pltpu.SMEM),
            pl.BlockSpec((comps, depth, wide), lambda i: (0, 0, i)),
            pl.BlockSpec((depth, wide), lambda i: (0, i)),
            pl.BlockSpec((depth, wide), lambda i: (0, i)),
            pl.BlockSpec((tiles, 2, LANES), lambda i: (i, 0, 0)),
        ],
        out_specs=(
            pl.BlockSpec((tiles, 32, LANES), lambda i: (i, 0, 0)),
            pl.BlockSpec((comps, depth, wide), lambda i: (0, 0, i)),
            pl.BlockSpec((2, depth, wide), lambda i: (0, 0, i)),
        ),
        interpret=INTERPRET,
        name="eliminate",
    )(first, class_cond, conc, porosity, cell_cond, meta)
    recv = lax.all_to_all(send, "col", split_axis=0, concat_axis=0, tiled=True)

    table = jnp.concatenate(
        [sorb_affinity.T, sorb_capacity[None], jnp.zeros((15 - comps, 16), F32)], axis=0
    )
    sorb = call(lookup_kernel, sds((owners, 16, LANES), F32), 2, name="lookup")(table, meta)

    ends, top = call(
        interface_kernel,
        (sds((owners * 24, LANES), F32), sds((groups, 16, LANES), F32)),
        3,
        name="interface",
    )(recv.reshape(owners * 32, LANES), surf_recv, active.reshape(1, LANES))
    ends = lax.all_to_all(
        ends.reshape(owners, 24, LANES), "col", split_axis=0, concat_axis=0, tiled=True
    )
    top = lax.all_to_all(top, "grp", split_axis=0, concat_axis=0, tiled=True)

    log_free = pl.pallas_call(
        speciate_kernel,
        grid=(steps,),
        out_shape=sds((comps, depth, width), F32),
        in_specs=[
            pl.BlockSpec((comps, depth, wide), lambda i: (0, 0, i)),
            pl.BlockSpec((2, depth, wide), lambda i: (0, 0, i)),
            pl.BlockSpec((depth, wide), lambda i: (0, i)),
            pl.BlockSpec((tiles, 24, LANES), lambda i: (i, 0, 0)),
            pl.BlockSpec((tiles, 16, LANES), lambda i: (i, 0, 0)),
        ],
        out_specs=pl.BlockSpec((comps, depth, wide), lambda i: (0, 0, i)),
        interpret=INTERPRET,
        name="speciate",
    )(g, vw, porosity, ends, sorb)

    flux = call(surf_flux_kernel, sds((comps, n), F32), 5, name="surf_flux")(
        top, surf_conc, rate, group, local
    )
    return (log_free, flux)


def solution(mesh):
    return jax.shard_map(
        body,
        mesh=mesh,
        in_specs=(
            P(None, "col", "grp"),
            P("col", "grp"),
            P("col", "grp"),
            P(("grp", "col")),
            P(("grp", "col")),
            P(),
            P(),
            P(),
            P(None, ("grp", "col")),
            P(("grp", "col")),
            P(("grp", "col"), None),
            P(("grp", "col")),
        ),
        out_specs=(P(None, "col", "grp"), P(None, ("grp", "col"))),
        check_vma=False,
    )
```

profile of v0, /device:TPU:64, one launch (start us, length us, event | category | flops | bytes accessed | tf_op | source)
XLA Modules:
  0.0 110.3 jit_solution(4169114552668595660)
XLA Ops:
  0.6 0.7 pad_add_fusion
  1.3 0.6 broadcast_in_dim.12
  1.9 12.6 %all-to-all-start = ((s32[32,2,128]{2,1,0:T(2,128)}), s32[32,2,128]{2,1,0:T(2,128)S(1)}, u32[]{:S(2)}, u32[]{:S(2)}) async-start(s32[32,2,128]{2,1,0:T(2,128)} %broadcast_in_dim.12), calls=%async_computation | async-start | bytes 65536 | tf_op jit(solution)/shard_map/all_to_all | solution.py:333
  14.5 1.8 %surf_pack.1 = f32[16,16,128]{2,1,0:T(8,128)} custom-call(f32[12,512]{1,0:T(8,128)} %conc_ref.5, f32[1,512]{1,0:T(1,128)} %bitcast.13, s32[1,512]{1,0:T(1,128)} %bitcast.15, s32[1,512]{1,0:T(1,128)} %bitcast.17), custom_call_target="tpu_custom_call" | custom-call | tf_op jit(solution)/shard_map/surf_pack/pallas_call | solution.py:338
  16.3 7.0 %all-to-all-done.meta_ref = s32[32,2,128]{2,1,0:T(2,128)S(1)} async-done(((s32[32,2,128]{2,1,0:T(2,128)}), s32[32,2,128]{2,1,0:T(2,128)S(1)}, u32[]{:S(2)}, u32[]{:S(2)}) %all-to-all-start) | async-done | bytes 32800 | tf_op jit(solution)/shard_map/all_to_all | solution.py:333
  23.4 7.2 %all-to-all-start.2 = ((f32[16,16,128]{2,1,0:T(8,128)}), f32[16,16,128]{2,1,0:T(8,128)S(1)}, u32[]{:S(2)}, u32[]{:S(2)}) async-start(f32[16,16,128]{2,1,0:T(8,128)} %surf_pack.1), calls=%async_computation.2 | async-start | bytes 262144 | tf_op jit(solution)/shard_map/all_to_all | solution.py:345
  30.6 0.0 copy-done.2
  30.6 6.4 %eliminate.1 = (f32[32,32,128]{2,1,0:T(8,128)}, f32[12,8,4096]{2,1,0:T(8,128)}, f32[2,8,4096]{2,1,0:T(8,128)}) custom-call(s32[1]{0:T(128)} %bitcast.first_ref, f32[16]{0:T(128)} %table_ref.1, f32[12,8,4096]{2,1,0:T(8,128)} %conc_ref.3, f32[8,4096]{1,0:T(8,128)} %theta_ref.3, f32[8,4096]{1,0:T(8,128)} %cond_ref.1, s32[32,2,128]{2,1,0:T(2,128)} %copy-done.2), custom_call_target="tpu_custom_call" | custom-call | tf_op jit(solution)/shard_map/eliminate/pallas_call | solution.py:350
  37.0 0.0 copy-start.4
  37.1 2.2 %all-to-all-done.2.surf_ref = f32[16,16,128]{2,1,0:T(8,128)S(1)} async-done(((f32[16,16,128]{2,1,0:T(8,128)}), f32[16,16,128]{2,1,0:T(8,128)S(1)}, u32[]{:S(2)}, u32[]{:S(2)}) %all-to-all-start.2) | async-done | bytes 131104 | tf_op jit(solution)/shard_map/all_to_all | solution.py:345
  39.2 24.2 %all_to_all.25 = f32[32,32,128]{2,1,0:T(8,128)} all-to-all(f32[32,32,128]{2,1,0:T(8,128)} %get-tuple-element.9), channel_id=1, replica_groups=mesh['grp'=16,'col'=32] {'col'}, dimensions={0} | all-to-all | bytes 1048576 | tf_op jit(solution)/shard_map/all_to_all | solution.py:374
  63.4 0.0 copy-done.1
  63.4 2.5 %interface.1 = (f32[768,128]{1,0:T(8,128)}, f32[16,16,128]{2,1,0:T(8,128)}) custom-call(f32[1024,128]{1,0:T(8,128)} %bitcast.10, f32[16,16,128]{2,1,0:T(8,128)} %copy-done.1, s32[1,128]{1,0:T(1,128)} %bitcast.20), custom_call_target="tpu_custom_call" | custom-call | tf_op jit(solution)/shard_map/interface/pallas_call | solution.py:381
  65.9 13.5 %all_to_all.26.table_ref = f32[16,16,128]{2,1,0:T(8,128)} all-to-all(f32[16,16,128]{2,1,0:T(8,128)} %get-tuple-element.11), channel_id=1, replica_groups=mesh['grp'=16,'col'=32] {'grp'}, dimensions={0} | all-to-all | bytes 262144 | tf_op jit(solution)/shard_map/all_to_all | solution.py:390
  79.4 4.9 %all-to-all-start.3 = ((f32[32,24,128]{2,1,0:T(8,128)}), f32[32,24,128]{2,1,0:T(8,128)S(1)}, u32[]{:S(2)}, u32[]{:S(2)}) async-start(f32[32,24,128]{2,1,0:T(8,128)} %bitcast.11), calls=%async_computation.3 | async-start | bytes 786432 | tf_op jit(solution)/shard_map/all_to_all | solution.py:387
  84.3 0.0 copy-done.3
  84.3 0.1 copy.14
  84.4 0.1 pad.2.clone
  84.5 0.7 maximum_maximum_fusion.table_ref
  85.1 1.9 %lookup.1.sorb_ref = f32[32,16,128]{2,1,0:T(8,128)} custom-call(f32[16,16]{1,0:T(8,128)} %maximum_maximum_fusion.table_ref, s32[32,2,128]{2,1,0:T(2,128)} %copy-done.2), custom_call_target="tpu_custom_call" | custom-call | tf_op jit(solution)/shard_map/lookup/pallas_call | solution.py:379
  87.0 1.9 %surf_flux.1 = f32[12,512]{1,0:T(8,128)} custom-call(f32[16,16,128]{2,1,0:T(8,128)} %all_to_all.26.table_ref, f32[12,512]{1,0:T(8,128)} %conc_ref.5, f32[1,512]{1,0:T(1,128)} %bitcast.14, s32[1,512]{1,0:T(1,128)} %bitcast.16, s32[1,512]{1,0:T(1,128)} %bitcast.18), custom_call_target="tpu_custom_call" | custom-call | tf_op jit(solution)/shard_map/surf_flux/pallas_call | solution.py:408
  88.9 10.8 %all-to-all-done.3.ends_ref = f32[32,24,128]{2,1,0:T(8,128)S(1)} async-done(((f32[32,24,128]{2,1,0:T(8,128)}), f32[32,24,128]{2,1,0:T(8,128)S(1)}, u32[]{:S(2)}, u32[]{:S(2)}) %all-to-all-start.3) | async-done | bytes 393248 | tf_op jit(solution)/shard_map/all_to_all | solution.py:387
  99.8 0.7 copy-done
  100.5 9.8 %speciate.1 = f32[12,8,4096]{2,1,0:T(8,128)} custom-call(f32[12,8,4096]{2,1,0:T(8,128)} %get-tuple-element.7.g_ref, f32[2,8,4096]{2,1,0:T(8,128)} %get-tuple-element.8.vw_ref, f32[8,4096]{1,0:T(8,128)} %theta_ref.3, f32[32,24,128]{2,1,0:T(8,128)} %copy-done, f32[32,16,128]{2,1,0:T(8,128)} %lookup.1.sorb_ref), custom_call_target="tpu_custom_call" | custom-call | tf_op jit(solution)/shard_map/speciate/pallas_call | solution.py:392
  (6 shorter events, 0.0 us)
Async XLA Ops:
  1.9 21.4 %all-to-all-start = ((s32[32,2,128]{2,1,0:T(2,128)}), s32[32,2,128]{2,1,0:T(2,128)S(1)}, u32[]{:S(2)}, u32[]{:S(2)}) async-start(s32[32,2,128]{2,1,0:T(2,128)} %broadcast_in_dim.12), calls=%async_computation | async-start | bytes 65536 | tf_op jit(solution)/shard_map/all_to_all | solution.py:333
  23.4 7.2 %copy-start.2 = (s32[32,2,128]{2,1,0:T(2,128)}, s32[32,2,128]{2,1,0:T(2,128)S(1)}, u32[]{:S(2)}) copy-start(s32[32,2,128]{2,1,0:T(2,128)S(1)} %all-to-all-done.meta_ref) | copy-start | bytes 98308
  23.4 15.9 %all-to-all-start.2 = ((f32[16,16,128]{2,1,0:T(8,128)}), f32[16,16,128]{2,1,0:T(8,128)S(1)}, u32[]{:S(2)}, u32[]{:S(2)}) async-start(f32[16,16,128]{2,1,0:T(8,128)} %surf_pack.1), calls=%async_computation.2 | async-start | bytes 262144 | tf_op jit(solution)/shard_map/all_to_all | solution.py:345
  37.0 47.2 %copy-start.3 = (f32[16,12]{1,0:T(8,128)S(1)}, f32[16,12]{1,0:T(8,128)}, u32[]{:S(2)}) copy-start(f32[16,12]{1,0:T(8,128)} %param.18) | copy-start | bytes 2308
  37.0 47.4 %copy-start.4 = (f32[16]{0:T(128)S(1)}, f32[16]{0:T(128)}, u32[]{:S(2)}) copy-start(f32[16]{0:T(128)} %param.19) | copy-start | bytes 196
  39.2 24.2 %copy-start.1 = (f32[16,16,128]{2,1,0:T(8,128)}, f32[16,16,128]{2,1,0:T(8,128)S(1)}, u32[]{:S(2)}) copy-start(f32[16,16,128]{2,1,0:T(8,128)S(1)} %all-to-all-done.2.surf_ref) | copy-start | bytes 393220
  79.4 20.4 %all-to-all-start.3 = ((f32[32,24,128]{2,1,0:T(8,128)}), f32[32,24,128]{2,1,0:T(8,128)S(1)}, u32[]{:S(2)}, u32[]{:S(2)}) async-start(f32[32,24,128]{2,1,0:T(8,128)} %bitcast.11), calls=%async_computation.3 | async-start | bytes 786432 | tf_op jit(solution)/shard_map/all_to_all | solution.py:387
  99.8 0.7 copy-start
where the time goes:
time: 111 us; the launch traced here: 110 us
  blocking collectives  37.7 us (34%)
  starting transfers between devices  24.6 us (22%)
  Pallas kernels  24.3 us (22%)
  waiting for transfers between devices  20 us (18%)
  local copies, waits for them, and re-layouts  1.54 us (1%)
  other arithmetic  1.35 us (1%)
    all_to_all x1, blocking collectives, body(): recv = lax.all_to_all(send, 'col', split_axis=0, concat_axis=0, tiled=True)  24.2 us
    all_to_all x1, blocking collectives, body(): top = lax.all_to_all(top, 'grp', split_axis=0, concat_axis=0, tiled=True)  13.5 us
    all_to_all x1, starting transfers between devices, body(): meta = lax.all_to_all(meta, 'col', split_axis=0, concat_axis=0, tiled=True)  12.6 us
    all_to_all x1, waiting for transfers between devices, body(): lax.all_to_all(ends.reshape(owners, 24, LANES), 'col', split_axis=0, conc...  10.8 us
    pallas_call x1, Pallas kernels, body(): pl.pallas_call(speciate_kernel, grid=(steps,), out_shape=sds((comps, dept...  9.76 us
    all_to_all x1, starting transfers between devices, body(): lax.all_to_all(surf_send, 'grp', split_axis=0, concat_axis=0, tiled=True)  7.21 us
    all_to_all x1, waiting for transfers between devices, body(): meta = lax.all_to_all(meta, 'col', split_axis=0, concat_axis=0, tiled=True)  7.02 us
    pallas_call x1, Pallas kernels, body(): pl.pallas_call(eliminate_kernel, grid=(steps,), out_shape=(sds((owners, 3...  6.45 us
  transfers between devices with their start and end apart: 3, of which 3 were waited for; matrix products, arithmetic and copies ran while one was open for 1% of the time, Pallas kernels for 11%

commit v1 on v0

--- a/solution.py
+++ b/solution.py
@@ -1,4 +1,3 @@
-import functools
 import jax
 import jax.numpy as jnp
 from jax import lax
@@ -66,9 +65,40 @@
 
 
 def eliminate_kernel(
-    first_ref, table_ref, conc_ref, theta_ref, cond_ref, meta_ref, send_ref, g_ref, vw_ref
+    first_ref,
+    table_ref,
+    conc_hbm,
+    theta_hbm,
+    cond_hbm,
+    meta_ref,
+    send_ref,
+    g_ref,
+    vw_ref,
+    conc_ref,
+    theta_ref,
+    cond_ref,
+    sems,
 ):
     comps = conc_ref.shape[0]
+    wide = conc_ref.shape[2] // CHUNKS
+
+    def in_copies(n):
+        part = pl.ds(pl.multiple_of(n * wide, wide), wide)
+        return [
+            pltpu.make_async_copy(
+                theta_hbm.at[:, part], theta_ref.at[:, part], sems.at[3 * n]
+            ),
+            pltpu.make_async_copy(
+                cond_hbm.at[:, part], cond_ref.at[:, part], sems.at[3 * n + 1]
+            ),
+            pltpu.make_async_copy(
+                conc_hbm.at[:, :, part], conc_ref.at[:, :, part], sems.at[3 * n + 2]
+            ),
+        ]
+
+    for n in range(CHUNKS):
+        for copy in in_copies(n):
+            copy.start()
     tiles = send_ref.shape[0]
     shape = (8, LANES)
     row = rows_iota(shape)
@@ -78,8 +108,8 @@
     def roll(v, d):
         return pltpu.roll(v, d % 8, 0)
 
-    for t in range(tiles):
-        cols = pl.ds(t * LANES, LANES)
+    def tile(t):
+        cols = pl.ds(pl.multiple_of(t * LANES, LANES), LANES)
         classes = meta_ref[t, 0:1, :]
         active = meta_ref[t, 1:2, :]
         scale = jnp.zeros((1, LANES), F32)
@@ -157,6 +187,24 @@
         send_ref[t, 0:8, :] = firsts
         send_ref[t, 8:16, :] = lasts
         send_ref[t, 16:24, :] = mixed
+
+    def tiles_of(i, carry):
+        for k in range(FEW):
+            tile(i * FEW + k)
+        return carry
+
+    per = tiles // FEW // CHUNKS
+
+    def chunk(n, carry):
+        for copy in in_copies(n):
+            copy.wait()
+        lax.fori_loop(n * per, (n + 1) * per, tiles_of, 0)
+        return carry
+
+    lax.fori_loop(0, CHUNKS, chunk, 0)
+
+
+FEW = 4
 
 
 def first_row(j):
@@ -236,55 +284,95 @@
         )
 
 
-def speciate_kernel(g_ref, vw_ref, theta_ref, ends_ref, sorb_ref, out_ref):
+LOG2E = 1.4426950408889634
+LN2 = 0.6931471805599453
+
+
+def tree_sum(terms):
+    while len(terms) > 1:
+        terms = [
+            terms[i] + terms[i + 1] if i + 1 < len(terms) else terms[i]
+            for i in range(0, len(terms), 2)
+        ]
+    return terms[0]
+
+
+def speciate_kernel(
+    g_ref, vw_ref, theta_ref, ends_ref, sorb_ref, log_ref, out_ref, sems
+):
     comps = g_ref.shape[0]
     tiles = ends_ref.shape[0]
-
-    def tile(t, carry):
-        cols = pl.ds(pl.multiple_of(t * LANES, LANES), LANES)
-        theta = theta_ref[:, cols]
-        v = vw_ref[0, :, cols]
-        w = vw_ref[1, :, cols]
-        cap = sorb_ref[t, comps : comps + 1, :]
-        aff = [sorb_ref[t, j : j + 1, :] for j in range(comps)]
-        sorb = [cap * a for a in aff]
-        x, c, p, at = [], [], [], []
-        for j in range(comps):
-            total = (
-                g_ref[j, :, cols]
-                + v * ends_ref[t, j : j + 1, :]
-                + w * ends_ref[t, 12 + j : 13 + j, :]
-            )
-            whole = theta + sorb[j]
-            start = total / whole
-            x.append(jnp.log(start))
-            c.append(start)
-            p.append(whole)
-            at.append(aff[j] * total)
+    each = range(comps)
+    wide = tiles * LANES // CHUNKS
+
+    def out_copy(n):
+        part = pl.ds(pl.multiple_of(n * wide, wide), wide)
+        return pltpu.make_async_copy(
+            out_ref.at[:, :, part], log_ref.at[:, :, part], sems.at[n]
+        )
+
+    def tile(i, carry):
+        group = [i * PAIR + k for k in range(PAIR)]
+        cells = range(len(group))
+        cols = [pl.ds(pl.multiple_of(t * LANES, LANES), LANES) for t in group]
+        theta = [theta_ref[:, n] for n in cols]
+        c = [[None] * comps for _ in cells]
+        p = [[None] * comps for _ in cells]
+        at = [[None] * comps for _ in cells]
+
+        def aff(k, j):
+            return sorb_ref[group[k], j : j + 1, :]
+
+        cap = [sorb_ref[t, comps : comps + 1, :] for t in group]
+        for j in each:
+            for k in cells:
+                total = (
+                    g_ref[j, :, cols[k]]
+                    + vw_ref[0, :, cols[k]] * ends_ref[group[k], j : j + 1, :]
+                    + vw_ref[1, :, cols[k]] * ends_ref[group[k], 12 + j : 13 + j, :]
+                )
+                whole = theta[k] + cap[k] * aff(k, j)
+                c[k][j] = total / whole
+                p[k][j] = whole
+                at[k][j] = aff(k, j) * total
         for step in range(ITERS):
-            ac = [aff[j] * c[j] for j in range(comps)]
-            load = sum(ac[1:], ac[0])
-            crowd = 1.0 + load
-            hold = theta * crowd
-            q = [1.0 / (hold + sorb[j]) for j in range(comps)]
-            sq = [sorb[j] * q[j] for j in range(comps)]
-            atq = [at[j] * q[j] for j in range(comps)]
-            acq = [ac[j] * sq[j] for j in range(comps)]
-            numer = load - crowd * sum(atq[1:], atq[0])
-            lean = sum(acq[1:], acq[0])
-            gain = 1.0 + numer / (crowd - lean)
-            for j in range(comps):
-                move = (theta - p[j]) * crowd * q[j] + sq[j] * gain
-                move = jnp.clip(move, -1.0, 1.0)
-                x[j] = x[j] - move
-                if step < ITERS - 1:
-                    c[j] = c[j] * jnp.exp(-move)
-                    p[j] = p[j] * jnp.exp(move)
-        for j in range(comps):
-            out_ref[j, :, cols] = x[j]
+            for k in cells:
+                ac = [aff(k, j) * c[k][j] for j in each]
+                load = tree_sum(ac)
+                crowd = 1.0 + load
+                hold = theta[k] * crowd
+                q = [1.0 / (hold + cap[k] * aff(k, j)) for j in each]
+                sum_c = tree_sum([ac[j] * q[j] for j in each])
+                sum_t = tree_sum([at[k][j] * q[j] for j in each])
+                lift = (load - crowd * sum_t) / (1.0 + hold * sum_c) * LOG2E
+                crowd = crowd * LOG2E
+                held = hold * lift
+                lift = lift + LOG2E
+                for j in each:
+                    move = q[j] * (p[k][j] * crowd + held) - lift
+                    move = jnp.clip(move, -LOG2E, LOG2E)
+                    if step < ITERS - 1:
+                        grow = jnp.exp2(move)
+                        c[k][j] = c[k][j] * grow
+                        p[k][j] = p[k][j] / grow
+                    else:
+                        out_ref[j, :, cols[k]] = jnp.log(c[k][j]) + move * LN2
         return carry
 
-    lax.fori_loop(0, tiles, tile, 0)
+    per = tiles // PAIR // CHUNKS
+
+    def chunk(n, carry):
+        lax.fori_loop(n * per, (n + 1) * per, tile, 0)
+        out_copy(n).start()
+        return carry
+
+    lax.fori_loop(0, CHUNKS, chunk, 0)
+    for n in range(CHUNKS):
+        out_copy(n).wait()
+
+
+PAIR = 2
+CHUNKS = 4
 
 
 VMEM = pltpu.VMEM
@@ -292,22 +380,36 @@
 
 def full(memory_space=VMEM):
     return pl.BlockSpec(memory_space=memory_space)
+
+
+def near(x):
+    return x if INTERPRET else pltpu.with_memory_space_constraint(x, VMEM)
+
+
+def held(shape):
+    return jax.ShapeDtypeStruct(shape, F32) if INTERPRET else VMEM(shape, F32)
 
 
 def call(kernel, out_shape, n_in, **kw):
     n_out = len(out_shape) if isinstance(out_shape, (tuple, list)) else None
     out_specs = full() if n_out is None else tuple(full() for _ in range(n_out))
-    return pl.pallas_call(
+    inner = pl.pallas_call(
         kernel,
         out_shape=out_shape,
         in_specs=[full()] * n_in,
         out_specs=out_specs,
         interpret=INTERPRET,
+        compiler_params=pltpu.CompilerParams(vmem_limit_bytes=24 << 20),
         **kw,
     )
-
-
-def body(
+    return lambda *args: inner(*(near(a) for a in args))
+
+
+def exchange(x, axis):
+    return lax.all_to_all(x, axis, split_axis=0, concat_axis=0, tiled=True)
+
+
+def step(
     conc,
     porosity,
     cell_cond,
@@ -328,82 +430,71 @@
     sds = jax.ShapeDtypeStruct
     first = (lax.axis_index("col") * depth).astype(jnp.int32).reshape(1)
 
-    meta = jnp.stack([soil_class, active])
-    meta = jnp.broadcast_to(meta[None], (owners, 2, LANES))
-    meta = lax.all_to_all(meta, "col", split_axis=0, concat_axis=0, tiled=True)
+    kind = lax.broadcasted_iota(jnp.int32, (owners, 2, LANES), 1)
+    meta = jnp.where(kind == 0, soil_class[None, None], active[None, None])
+    meta = exchange(meta, "col")
 
     rate = surf_rate.reshape(1, n)
     group = surf_group.reshape(1, n)
     local = surf_local.reshape(1, n)
     surf_send = call(
         surf_pack_kernel,
-        sds((groups, 16, LANES), F32),
+        held((groups, 16, LANES)),
         4,
         scratch_shapes=[pltpu.VMEM((3, 16 * groups, n), jnp.bfloat16)],
         name="surf_pack",
     )(surf_conc, rate, group, local)
-    surf_recv = lax.all_to_all(surf_send, "grp", split_axis=0, concat_axis=0, tiled=True)
-
-    tiles = 4
-    steps = owners // tiles
-    wide = tiles * LANES
+    surf_recv = exchange(surf_send, "grp")
+
+    smem = pl.BlockSpec(memory_space=pltpu.SMEM)
     send, g, vw = pl.pallas_call(
         eliminate_kernel,
-        grid=(steps,),
         out_shape=(
-            sds((owners, 32, LANES), F32),
-            sds((comps, depth, width), F32),
-            sds((2, depth, width), F32),
+            held((owners, 32, LANES)),
+            held((comps, depth, width)),
+            held((2, depth, width)),
         ),
-        in_specs=[
-            pl.BlockSpec(memory_space=pltpu.SMEM),
-            pl.BlockSpec(memory_space=pltpu.SMEM),
-            pl.BlockSpec((comps, depth, wide), lambda i: (0, 0, i)),
-            pl.BlockSpec((depth, wide), lambda i: (0, i)),
-            pl.BlockSpec((depth, wide), lambda i: (0, i)),
-            pl.BlockSpec((tiles, 2, LANES), lambda i: (i, 0, 0)),
+        in_specs=[smem, smem] + [pl.BlockSpec(memory_space=pl.ANY)] * 3 + [full()],
+        out_specs=(full(), full(), full()),
+        scratch_shapes=[
+            pltpu.VMEM((comps, depth, width), F32),
+            pltpu.VMEM((depth, width), F32),
+            pltpu.VMEM((depth, width), F32),
+            pltpu.SemaphoreType.DMA((3 * CHUNKS,)),
         ],
-        out_specs=(
-            pl.BlockSpec((tiles, 32, LANES), lambda i: (i, 0, 0)),
-            pl.BlockSpec((comps, depth, wide), lambda i: (0, 0, i)),
-            pl.BlockSpec((2, depth, wide), lambda i: (0, 0, i)),
-        ),
         interpret=INTERPRET,
+        compiler_params=pltpu.CompilerParams(vmem_limit_bytes=24 << 20),
         name="eliminate",
-    )(first, class_cond, conc, porosity, cell_cond, meta)
-    recv = lax.all_to_all(send, "col", split_axis=0, concat_axis=0, tiled=True)
+    )(first, class_cond, conc, porosity, cell_cond, near(meta))
+    recv = exchange(send, "col")
 
     table = jnp.concatenate(
         [sorb_affinity.T, sorb_capacity[None], jnp.zeros((15 - comps, 16), F32)], axis=0
     )
-    sorb = call(lookup_kernel, sds((owners, 16, LANES), F32), 2, name="lookup")(table, meta)
+    sorb = call(lookup_kernel, held((owners, 16, LANES)), 2, name="lookup")(table, meta)
 
     ends, top = call(
         interface_kernel,
-        (sds((owners * 24, LANES), F32), sds((groups, 16, LANES), F32)),
+        (held((owners * 24, LANES)), held((groups, 16, LANES))),
         3,
         name="interface",
     )(recv.reshape(owners * 32, LANES), surf_recv, active.reshape(1, LANES))
-    ends = lax.all_to_all(
-        ends.reshape(owners, 24, LANES), "col", split_axis=0, concat_axis=0, tiled=True
-    )
-    top = lax.all_to_all(top, "grp", split_axis=0, concat_axis=0, tiled=True)
+    ends = exchange(ends.reshape(owners, 24, LANES), "col")
+    top = exchange(top, "grp")
 
     log_free = pl.pallas_call(
         speciate_kernel,
-        grid=(steps,),
         out_shape=sds((comps, depth, width), F32),
-        in_specs=[
-            pl.BlockSpec((comps, depth, wide), lambda i: (0, 0, i)),
-            pl.BlockSpec((2, depth, wide), lambda i: (0, 0, i)),
-            pl.BlockSpec((depth, wide), lambda i: (0, i)),
-            pl.BlockSpec((tiles, 24, LANES), lambda i: (i, 0, 0)),
-            pl.BlockSpec((tiles, 16, LANES), lambda i: (i, 0, 0)),
+        in_specs=[full()] * 5,
+        out_specs=pl.BlockSpec(memory_space=pl.ANY),
+        scratch_shapes=[
+            pltpu.VMEM((comps, depth, width), F32),
+            pltpu.SemaphoreType.DMA((CHUNKS,)),
         ],
-        out_specs=pl.BlockSpec((comps, depth, wide), lambda i: (0, 0, i)),
         interpret=INTERPRET,
+        compiler_params=pltpu.CompilerParams(vmem_limit_bytes=24 << 20),
         name="speciate",
-    )(g, vw, porosity, ends, sorb)
+    )(near(g), near(vw), near(porosity), near(ends), near(sorb))
 
     flux = call(surf_flux_kernel, sds((comps, n), F32), 5, name="surf_flux")(
         top, surf_conc, rate, group, local
@@ -413,7 +504,7 @@
 
 def solution(mesh):
     return jax.shard_map(
-        body,
+        step,
         mesh=mesh,
         in_specs=(
             P(None, "col", "grp"),

time: 111 us -> 105 us (0.946)
  Pallas kernels: 24.3 us -> 12.9 us
  local copies, waits for them, and re-layouts: 1.54 us -> 6.88 us
    pallas_call x6, Pallas kernels: 24.3 us -> 12.9 us  [the longest x1 5.6 us: step(): pl.pallas_call(speciate_kernel, out_shape=sds((comps, depth, width), F32)...]
    unnamed x11 -> x33, local copies, waits for them, and re-layouts: 0.84 us -> 6.8 us
    select_n x0 -> x1, other arithmetic: none -> 1.37 us  [step(): meta = jnp.where(kind == 0, soil_class[None, None], active[None, None])]
  transfers between devices with their start and end apart: 3 -> 3, of which waited for: 3 -> 3; matrix products, arithmetic and copies ran while one was open for 1% -> 0% of each run, Pallas kernels for 11% -> 6%
where the time goes in v1:
time: 105 us; the launch traced here: 104 us
  blocking collectives  37.3 us (36%)
  starting transfers between devices  24.6 us (23%)
  waiting for transfers between devices  19.9 us (19%)
  Pallas kernels  12.9 us (12%)
  local copies, waits for them, and re-layouts  6.88 us (7%)
  other arithmetic  1.45 us (1%)
    all_to_all x2, blocking collectives, exchange(): return lax.all_to_all(x, axis, split_axis=0, concat_axis=0, tiled=True)  37.3 us
    all_to_all x3, starting transfers between devices, exchange(): return lax.all_to_all(x, axis, split_axis=0, concat_axis=0, tiled=True)  24.6 us
    all_to_all x3, waiting for transfers between devices, exchange(): return lax.all_to_all(x, axis, split_axis=0, concat_axis=0, tiled=True)  19.9 us
    unnamed x33, local copies, waits for them, and re-layouts  6.8 us
    pallas_call x1, Pallas kernels, step(): pl.pallas_call(speciate_kernel, out_shape=sds((comps, depth, width), F32)...  5.6 us
    pallas_call x4, Pallas kernels, call(): return lambda *args: inner(*(near(a) for a in args))  3.78 us
    pallas_call x1, Pallas kernels, step(): pl.pallas_call(eliminate_kernel, out_shape=(held((owners, 32, LANES)), he...  3.57 us
  transfers between devices with their start and end apart: 3, of which 3 were waited for; matrix products, arithmetic and copies ran while one was open for 0% of the time, Pallas kernels for 6%

profile of v1, /device:TPU:64, one launch (start us, length us, event | category | flops | bytes accessed | tf_op | source)
XLA Modules:
  0.0 103.9 jit_solution(3911594555771777454)
XLA Ops:
  0.6 1.4 %broadcast_select_fusion = s32[32,2,128]{2,1,0:T(2,128)} fusion(pred[2]{0:T(512)(128)(4,1)S(1)} %iota_compare_fusion, s32[128]{0:T(128)} %param.16, s32[128]{0:T(128)} %param.15), kind=kLoop, calls=%fused_computation | loop fusion | flops 8192 | bytes 33794 | tf_op jit(solution)/shard_map/jit(_where)/select_n | solution.py:434
  2.0 12.6 %all-to-all-start = ((s32[32,2,128]{2,1,0:T(2,128)}), s32[32,2,128]{2,1,0:T(2,128)S(1)}, u32[]{:S(2)}, u32[]{:S(2)}) async-start(s32[32,2,128]{2,1,0:T(2,128)} %broadcast_select_fusion), calls=%async_computation | async-start | bytes 65536 | tf_op jit(solution)/shard_map/all_to_all | solution.py:409
  14.6 0.7 copy-done.4
  15.4 0.7 copy-done.6
  16.0 0.7 copy-done.8
  16.7 0.7 copy-done.10
  17.4 1.0 surf_pack.1
  18.4 5.0 %all-to-all-done.meta_ref = s32[32,2,128]{2,1,0:T(2,128)S(1)} async-done(((s32[32,2,128]{2,1,0:T(2,128)}), s32[32,2,128]{2,1,0:T(2,128)S(1)}, u32[]{:S(2)}, u32[]{:S(2)}) %all-to-all-start) | async-done | bytes 32800 | tf_op jit(solution)/shard_map/all_to_all | solution.py:409
  23.4 7.2 %all-to-all-start.2 = ((f32[16,16,128]{2,1,0:T(8,128)}), f32[16,16,128]{2,1,0:T(8,128)S(1)}, u32[]{:S(2)}, u32[]{:S(2)}) async-start(f32[16,16,128]{2,1,0:T(8,128)} %surf_pack.1), calls=%async_computation.2 | async-start | bytes 262144 | tf_op jit(solution)/shard_map/all_to_all | solution.py:409
  30.7 1.4 %copy-done = f32[12,8,4096]{2,1,0:T(8,128)S(1)} copy-done((f32[12,8,4096]{2,1,0:T(8,128)S(1)}, f32[12,8,4096]{2,1,0:T(8,128)}, u32[]{:S(2)}) %copy-start) | copy-done | bytes 1572888
  32.1 0.9 copy-done.1
  33.0 0.9 copy-done.3
  33.9 0.7 copy-done.13
  34.5 3.6 %eliminate.1 = (f32[32,32,128]{2,1,0:T(8,128)S(1)}, f32[12,8,4096]{2,1,0:T(8,128)S(1)}, f32[2,8,4096]{2,1,0:T(8,128)S(1)}) custom-call(s32[1]{0:T(128)} %bitcast.first_ref, f32[16]{0:T(128)S(1)} %copy-done.13, f32[12,8,4096]{2,1,0:T(8,128)S(1)} %copy-done, f32[8,4096]{1,0:T(8,128)S(1)} %copy-done.1, f32[8,4096]{1,0:T(8,128)S(1)} %copy-done.3, ...), custom_call_target="tpu_custom_call" | custom-call | tf_op jit(solution)/shard_map/eliminate/pallas_call | solution.py:450
  38.2 1.1 %all-to-all-done.2.surf_ref = f32[16,16,128]{2,1,0:T(8,128)S(1)} async-done(((f32[16,16,128]{2,1,0:T(8,128)}), f32[16,16,128]{2,1,0:T(8,128)S(1)}, u32[]{:S(2)}, u32[]{:S(2)}) %all-to-all-start.2) | async-done | bytes 131104 | tf_op jit(solution)/shard_map/all_to_all | solution.py:409
  39.3 23.3 %all_to_all.25 = f32[32,32,128]{2,1,0:T(8,128)S(1)} all-to-all(f32[32,32,128]{2,1,0:T(8,128)S(1)} %get-tuple-element.9), channel_id=1, replica_groups=mesh['grp'=16,'col'=32] {'col'}, dimensions={0} | all-to-all | bytes 1048576 | tf_op jit(solution)/shard_map/all_to_all | solution.py:409
  62.6 1.4 %interface.1 = (f32[768,128]{1,0:T(8,128)}, f32[16,16,128]{2,1,0:T(8,128)S(1)}) custom-call(f32[1024,128]{1,0:T(8,128)S(1)} %bitcast.9, f32[16,16,128]{2,1,0:T(8,128)S(1)} %all-to-all-done.2.surf_ref, s32[1,128]{1,0:T(1,128)S(1)} %bitcast.16), custom_call_target="tpu_custom_call" | custom-call | tf_op jit(solution)/shard_map/interface/pallas_call | solution.py:405
  64.0 14.0 %all_to_all.26.table_ref = f32[16,16,128]{2,1,0:T(8,128)S(1)} all-to-all(f32[16,16,128]{2,1,0:T(8,128)S(1)} %get-tuple-element.11), channel_id=1, replica_groups=mesh['grp'=16,'col'=32] {'grp'}, dimensions={0} | all-to-all | bytes 262144 | tf_op jit(solution)/shard_map/all_to_all | solution.py:409
  78.0 4.8 %all-to-all-start.3 = ((f32[32,24,128]{2,1,0:T(8,128)}), f32[32,24,128]{2,1,0:T(8,128)S(1)}, u32[]{:S(2)}, u32[]{:S(2)}) async-start(f32[32,24,128]{2,1,0:T(8,128)} %bitcast.6), calls=%async_computation.3 | async-start | bytes 786432 | tf_op jit(solution)/shard_map/all_to_all | solution.py:409
  82.9 0.1 copy.14
  83.1 0.4 lookup.1.sorb_ref
  83.5 1.0 surf_flux.1
  84.5 13.8 %all-to-all-done.3.ends_ref = f32[32,24,128]{2,1,0:T(8,128)S(1)} async-done(((f32[32,24,128]{2,1,0:T(8,128)}), f32[32,24,128]{2,1,0:T(8,128)S(1)}, u32[]{:S(2)}, u32[]{:S(2)}) %all-to-all-start.3) | async-done | bytes 393248 | tf_op jit(solution)/shard_map/all_to_all | solution.py:409
  98.3 5.6 %speciate.1 = f32[12,8,4096]{2,1,0:T(8,128)} custom-call(f32[12,8,4096]{2,1,0:T(8,128)S(1)} %get-tuple-element.7.g_ref, f32[2,8,4096]{2,1,0:T(8,128)S(1)} %get-tuple-element.8.vw_ref, f32[8,4096]{1,0:T(8,128)S(1)} %copy-done.2, f32[32,24,128]{2,1,0:T(8,128)S(1)} %all-to-all-done.3.ends_ref, f32[32,16,128]{2,1,0:T(8,128)S(1)} %lookup.1.sorb_ref), custom_call_target="tpu_custom_call" | custom-call | tf_op jit(solution)/shard_map/speciate/pallas_call | solution.py:485
  (28 shorter events, 0.2 us)
Async XLA Ops:
  2.0 21.4 %all-to-all-start = ((s32[32,2,128]{2,1,0:T(2,128)}), s32[32,2,128]{2,1,0:T(2,128)S(1)}, u32[]{:S(2)}, u32[]{:S(2)}) async-start(s32[32,2,128]{2,1,0:T(2,128)} %broadcast_select_fusion), calls=%async_computation | async-start | bytes 65536 | tf_op jit(solution)/shard_map/all_to_all | solution.py:409
  14.6 0.8 copy-start.4
  15.4 0.7 copy-start.6
  16.0 0.7 copy-start.8
  16.7 0.7 copy-start.10
  18.4 44.2 %copy-start.12 = (s32[128]{0:T(128)S(1)}, s32[128]{0:T(128)}, u32[]{:S(2)}) copy-start(s32[128]{0:T(128)} %param.16) | copy-start | bytes 1540
  23.4 15.9 %all-to-all-start.2 = ((f32[16,16,128]{2,1,0:T(8,128)}), f32[16,16,128]{2,1,0:T(8,128)S(1)}, u32[]{:S(2)}, u32[]{:S(2)}) async-start(f32[16,16,128]{2,1,0:T(8,128)} %surf_pack.1), calls=%async_computation.2 | async-start | bytes 262144 | tf_op jit(solution)/shard_map/all_to_all | solution.py:409
  30.6 1.4 %copy-start = (f32[12,8,4096]{2,1,0:T(8,128)S(1)}, f32[12,8,4096]{2,1,0:T(8,128)}, u32[]{:S(2)}) copy-start(f32[12,8,4096]{2,1,0:T(8,128)} %conc_hbm.1) | copy-start | bytes 4718596
  32.1 0.9 copy-start.1
  33.0 0.9 copy-start.3
  33.9 0.7 copy-start.13
  38.1 44.8 %copy-start.14 = (f32[16,12]{1,0:T(8,128)S(1)}, f32[16,12]{1,0:T(8,128)}, u32[]{:S(2)}) copy-start(f32[16,12]{1,0:T(8,128)} %param.18) | copy-start | bytes 2308
  38.1 44.9 %copy-start.15 = (f32[16]{0:T(128)S(1)}, f32[16]{0:T(128)}, u32[]{:S(2)}) copy-start(f32[16]{0:T(128)} %param.19) | copy-start | bytes 196
  38.1 45.4 %copy-start.5 = (f32[12,512]{1,0:T(8,128)S(1)}, f32[12,512]{1,0:T(8,128)}, u32[]{:S(2)}) copy-start(f32[12,512]{1,0:T(8,128)} %conc_ref.3) | copy-start | bytes 73732
  38.1 45.4 %copy-start.7 = (f32[512]{0:T(512)S(1)}, f32[512]{0:T(512)}, u32[]{:S(2)}) copy-start(f32[512]{0:T(512)} %param.21) | copy-start | bytes 6148
  38.1 45.4 %copy-start.9 = (s32[512,1]{0,1:T(1,128)S(1)}, s32[512,1]{0,1:T(1,128)}, u32[]{:S(2)}) copy-start(s32[512,1]{0,1:T(1,128)} %param.22) | copy-start | bytes 6148
  38.2 45.4 %copy-start.11 = (s32[512]{0:T(512)S(1)}, s32[512]{0:T(512)}, u32[]{:S(2)}) copy-start(s32[512]{0:T(512)} %param.23) | copy-start | bytes 6148
  39.3 59.1 %copy-start.2 = (f32[8,4096]{1,0:T(8,128)S(1)}, f32[8,4096]{1,0:T(8,128)}, u32[]{:S(2)}) copy-start(f32[8,4096]{1,0:T(8,128)} %theta_ref.1) | copy-start | bytes 393220
  78.0 20.3 %all-to-all-start.3 = ((f32[32,24,128]{2,1,0:T(8,128)}), f32[32,24,128]{2,1,0:T(8,128)S(1)}, u32[]{:S(2)}, u32[]{:S(2)}) async-start(f32[32,24,128]{2,1,0:T(8,128)} %bitcast.6), calls=%async_computation.3 | async-start | bytes 786432 | tf_op jit(solution)/shard_map/all_to_all | solution.py:409

commit v2 on v1

--- a/solution.py
+++ b/solution.py
@@ -23,45 +23,63 @@
     return lax.broadcasted_iota(jnp.int32, shape, 0)
 
 
-def surf_pack_kernel(conc_ref, rate_ref, group_ref, local_ref, send_ref, lhs_ref):
+def surf_pack_kernel(
+    me_ref, conc_ref, rate_ref, group_ref, local_ref, keep_ref, send_ref, lhs_ref
+):
     comps, n = conc_ref.shape
-    groups = send_ref.shape[0]
+    half = send_ref.shape[0]
     rate = rate_ref[...]
     vals = jnp.concatenate(
         [conc_ref[...] * rate, rate, jnp.zeros((15 - comps, n), F32)], axis=0
     )
-    hi, mid, lo = split3(vals)
-    group = group_ref[...]
-    for g in range(groups):
-        keep = group == g
-        for i, part in enumerate((hi, mid, lo)):
-            lhs_ref[i, 16 * g : 16 * g + 16, :] = jnp.where(
-                keep, part.astype(F32), 0.0
-            ).astype(jnp.bfloat16)
+    parts = [part.astype(F32) for part in split3(vals)]
+    slot = group_ref[...] ^ me_ref[0]
+    for b in range(2 * half):
+        keep = slot == b
+        for i, part in enumerate(parts):
+            lhs_ref[i, 16 * b : 16 * b + 16, :] = jnp.where(keep, part, 0.0).astype(
+                jnp.bfloat16
+            )
     place = (rows_iota((LANES, n)) == local_ref[...]).astype(F32).astype(jnp.bfloat16)
     dims = (((1,), (1,)), ((), ()))
     total = sum(
         lax.dot_general(lhs_ref[i], place, dims, preferred_element_type=F32)
         for i in (2, 1, 0)
     )
-    send_ref[...] = total.reshape(groups, 16, LANES)
-
-
-def surf_flux_kernel(table_ref, conc_ref, rate_ref, group_ref, local_ref, flux_ref):
+    total = total.reshape(2 * half, 16, LANES)
+    keep_ref[...] = total[:half]
+    send_ref[...] = total[half:]
+
+
+def surf_flux_kernel(
+    me_ref, near_ref, far_ref, conc_ref, rate_ref, group_ref, local_ref, flux_ref
+):
     comps, n = conc_ref.shape
-    groups = table_ref.shape[0]
-    table = table_ref[...].reshape(groups * 16, LANES)
+    half = far_ref.shape[0]
     place = (rows_iota((LANES, n)) == local_ref[...]).astype(F32).astype(jnp.bfloat16)
-    hi, mid, lo = split3(table)
+    table = jnp.concatenate([near_ref[...], far_ref[...]], axis=0)
+    hi, mid, lo = split3(table.reshape(2 * half * 16, LANES))
     picked = jnp.dot(lo, place, preferred_element_type=F32)
     picked += jnp.dot(mid, place, preferred_element_type=F32)
     picked += jnp.dot(hi, place, preferred_element_type=F32)
-    group = group_ref[...]
+    slot = group_ref[...] ^ me_ref[0]
     top = jnp.zeros((16, n), F32)
-    for g in range(groups):
-        top = jnp.where(group == g, picked[16 * g : 16 * g + 16], top)
+    for i in range(2 * half):
+        top = jnp.where(slot == slot_mask(i, 2 * half), picked[16 * i : 16 * i + 16], top)
     rate = rate_ref[...]
     flux_ref[...] = rate * conc_ref[...] - rate * top[:comps]
+
+
+def halvings(n):
+    masks = []
+    while n > 1:
+        n //= 2
+        masks.append(n)
+    return masks
+
+
+def slot_mask(i, n):
+    return sum(m for k, m in enumerate(halvings(n)) if i >> k & 1)
 
 
 def eliminate_kernel(
@@ -215,10 +233,10 @@
     return 8 + (j + 7) % 8 if j < 8 else 20 + j - 8
 
 
-def interface_kernel(recv_ref, surf_ref, active_ref, ends_ref, top_ref):
+def interface_kernel(recv_ref, active_ref, *refs):
+    *surf_refs, ends_ref, top_ref = refs
     blocks = ends_ref.shape[0] // 24
     comps = 12
-    groups = top_ref.shape[0]
     shape = (blocks, LANES)
     row = rows_iota(shape)
     zero = jnp.zeros(shape, F32)
@@ -229,9 +247,7 @@
     def take(r):
         return recv_ref[pl.ds(r, blocks, stride=32), :]
 
-    partial = surf_ref[0]
-    for g in range(1, surf_ref.shape[0]):
-        partial = partial + surf_ref[g]
+    partial = tree_sum([ref[0] for ref in surf_refs])
     alpha = take(24) + jnp.where(row == 0, partial[comps : comps + 1], zero)
     beta, cross, s_first, s_last = take(25), take(26), take(27), take(28)
     s_above = roll(s_last, 1)
@@ -265,9 +281,9 @@
         ends_ref[pl.ds(j, blocks, stride=24), :] = first
         ends_ref[pl.ds(12 + j, blocks, stride=24), :] = last
         tops.append(first[0:1])
-    top = jnp.concatenate(tops + [jnp.zeros((16 - comps, LANES), F32)], axis=0)
-    for g in range(groups):
-        top_ref[g] = top
+    top_ref[0] = jnp.concatenate(
+        tops + [jnp.zeros((16 - comps, LANES), F32)], axis=0
+    )
 
 
 def lookup_kernel(table_ref, meta_ref, out_ref):
@@ -375,7 +391,7 @@
 CHUNKS = 4
 
 
-VMEM = pltpu.VMEM
+VMEM, HBM = pltpu.VMEM, pltpu.HBM
 
 
 def full(memory_space=VMEM):
@@ -386,8 +402,17 @@
     return x if INTERPRET else pltpu.with_memory_space_constraint(x, VMEM)
 
 
+def far(x):
+    return x if INTERPRET else pltpu.with_memory_space_constraint(x, HBM)
+
+
 def held(shape):
     return jax.ShapeDtypeStruct(shape, F32) if INTERPRET else VMEM(shape, F32)
+
+
+def swap(x, mask):
+    n = lax.axis_size("grp")
+    return lax.ppermute(x, "grp", [(i, i ^ mask) for i in range(n)])
 
 
 def call(kernel, out_shape, n_in, **kw):
@@ -437,16 +462,29 @@
     rate = surf_rate.reshape(1, n)
     group = surf_group.reshape(1, n)
     local = surf_local.reshape(1, n)
-    surf_send = call(
+    smem = pl.BlockSpec(memory_space=pltpu.SMEM)
+    me = lax.axis_index("grp").astype(jnp.int32).reshape(1)
+    masks = halvings(groups)
+    keep, surf_send = pl.pallas_call(
         surf_pack_kernel,
-        held((groups, 16, LANES)),
-        4,
+        out_shape=(
+            sds((groups // 2, 16, LANES), F32),
+            sds((groups // 2, 16, LANES), F32),
+        ),
+        in_specs=[smem] + [full()] * 4,
+        out_specs=(full(), full()),
         scratch_shapes=[pltpu.VMEM((3, 16 * groups, n), jnp.bfloat16)],
+        interpret=INTERPRET,
+        compiler_params=pltpu.CompilerParams(vmem_limit_bytes=24 << 20),
         name="surf_pack",
-    )(surf_conc, rate, group, local)
-    surf_recv = exchange(surf_send, "grp")
-
-    smem = pl.BlockSpec(memory_space=pltpu.SMEM)
+    )(me, *(far(x) for x in (surf_conc, rate, group, local)))
+    surf_parts = [keep]
+    for k, mask in enumerate(masks):
+        if k:
+            surf_send = sum(x[mask : 2 * mask] for x in surf_parts)
+        surf_parts.append(swap(surf_send, mask))
+    surf_parts = [x[:1] for x in surf_parts]
+
     send, g, vw = pl.pallas_call(
         eliminate_kernel,
         out_shape=(
@@ -454,7 +492,7 @@
             held((comps, depth, width)),
             held((2, depth, width)),
         ),
-        in_specs=[smem, smem] + [pl.BlockSpec(memory_space=pl.ANY)] * 3 + [full()],
+        in_specs=[smem, smem] + [pl.BlockSpec(memory_space=HBM)] * 3 + [full()],
         out_specs=(full(), full(), full()),
         scratch_shapes=[
             pltpu.VMEM((comps, depth, width), F32),
@@ -465,7 +503,7 @@
         interpret=INTERPRET,
         compiler_params=pltpu.CompilerParams(vmem_limit_bytes=24 << 20),
         name="eliminate",
-    )(first, class_cond, conc, porosity, cell_cond, near(meta))
+    )(first, far(class_cond), far(conc), far(porosity), far(cell_cond), near(meta))
     recv = exchange(send, "col")
 
     table = jnp.concatenate(
@@ -475,12 +513,15 @@
 
     ends, top = call(
         interface_kernel,
-        (held((owners * 24, LANES)), held((groups, 16, LANES))),
-        3,
+        (held((owners * 24, LANES)), held((1, 16, LANES))),
+        2 + len(surf_parts),
         name="interface",
-    )(recv.reshape(owners * 32, LANES), surf_recv, active.reshape(1, LANES))
+    )(recv.reshape(owners * 32, LANES), active.reshape(1, LANES), *surf_parts)
     ends = exchange(ends.reshape(owners, 24, LANES), "col")
-    top = exchange(top, "grp")
+    for k, mask in enumerate(masks):
+        if k:
+            top = jnp.concatenate([top, other], axis=0)
+        other = swap(top, mask)
 
     log_free = pl.pallas_call(
         speciate_kernel,
@@ -496,9 +537,15 @@
         name="speciate",
     )(near(g), near(vw), near(porosity), near(ends), near(sorb))
 
-    flux = call(surf_flux_kernel, sds((comps, n), F32), 5, name="surf_flux")(
-        top, surf_conc, rate, group, local
-    )
+    flux = pl.pallas_call(
+        surf_flux_kernel,
+        out_shape=sds((comps, n), F32),
+        in_specs=[smem] + [full()] * 6,
+        out_specs=full(),
+        interpret=INTERPRET,
+        compiler_params=pltpu.CompilerParams(vmem_limit_bytes=24 << 20),
+        name="surf_flux",
+    )(me, near(top), near(other), *(near(x) for x in (surf_conc, rate, group, local)))
     return (log_free, flux)
 
 

time: 105 us -> 105 us (level)
  the two profiles are of different devices: /device:TPU:64 before, /device:TPU:1 now
where the time goes in v2:
time: 105 us; the launch traced here: 104 us
  starting transfers between devices  64.8 us (62%)
  waiting for transfers between devices  22 us (21%)
  Pallas kernels  14.7 us (14%)
  other arithmetic  1.47 us (1%)
    ppermute x8, starting transfers between devices, swap(): return lax.ppermute(x, 'grp', [(i, i ^ mask) for i in range(n)])  37.7 us
    all_to_all x3, starting transfers between devices, exchange(): return lax.all_to_all(x, axis, split_axis=0, concat_axis=0, tiled=True)  27.1 us
    ppermute x8, waiting for transfers between devices, swap(): return lax.ppermute(x, 'grp', [(i, i ^ mask) for i in range(n)])  13.2 us
    all_to_all x3, waiting for transfers between devices, exchange(): return lax.all_to_all(x, axis, split_axis=0, concat_axis=0, tiled=True)  8.77 us
    pallas_call x1, Pallas kernels, step(): pl.pallas_call(speciate_kernel, out_shape=sds((comps, depth, width), F32)...  5.6 us
    pallas_call x1, Pallas kernels, step(): pl.pallas_call(eliminate_kernel, out_shape=(held((owners, 32, LANES)), he...  5.19 us
  transfers between devices with their start and end apart: 11, of which 8 were waited for; matrix products, arithmetic and copies ran while one was open for 0% of the time, Pallas kernels for 2%

profile of v2, /device:TPU:1, one launch (start us, length us, event | category | flops | bytes accessed | tf_op | source)
XLA Modules:
  0.0 104.0 jit_solution(2917065291186981682)
XLA Ops:
  0.6 1.4 %broadcast_select_fusion = s32[32,2,128]{2,1,0:T(2,128)} fusion(pred[2]{0:T(512)(128)(4,1)S(1)} %iota_compare_fusion, s32[128]{0:T(128)} %param.16, s32[128]{0:T(128)} %param.15), kind=kLoop, calls=%fused_computation.2 | loop fusion | flops 8192 | bytes 33794 | tf_op jit(solution)/shard_map/jit(_where)/select_n | solution.py:459
  2.0 13.7 %all-to-all-start = ((s32[32,2,128]{2,1,0:T(2,128)}), s32[32,2,128]{2,1,0:T(2,128)S(1)}, u32[]{:S(2)}, u32[]{:S(2)}) async-start(s32[32,2,128]{2,1,0:T(2,128)} %broadcast_select_fusion), calls=%async_computation | async-start | bytes 65536 | tf_op jit(solution)/shard_map/all_to_all | solution.py:434
  15.7 8.8 %all-to-all-done.meta_ref = s32[32,2,128]{2,1,0:T(2,128)S(1)} async-done(((s32[32,2,128]{2,1,0:T(2,128)}), s32[32,2,128]{2,1,0:T(2,128)S(1)}, u32[]{:S(2)}, u32[]{:S(2)}) %all-to-all-start) | async-done | bytes 32800 | tf_op jit(solution)/shard_map/all_to_all | solution.py:434
  24.5 5.2 %eliminate.1 = (f32[32,32,128]{2,1,0:T(8,128)}, f32[12,8,4096]{2,1,0:T(8,128)S(1)}, f32[2,8,4096]{2,1,0:T(8,128)S(1)}) custom-call(s32[1]{0:T(128)} %bitcast.first_ref, f32[16]{0:T(128)} %table_ref.1, f32[12,8,4096]{2,1,0:T(8,128)} %conc_hbm.1, f32[8,4096]{1,0:T(8,128)} %theta_ref.1, f32[8,4096]{1,0:T(8,128)} %cond_hbm.1, ...), custom_call_target="tpu_custom_call" | custom-call | tf_op jit(solution)/shard_map/eliminate/pallas_call | solution.py:488
  29.8 4.0 %all-to-all-start.1 = ((f32[32,32,128]{2,1,0:T(8,128)}), f32[32,32,128]{2,1,0:T(8,128)S(1)}, u32[]{:S(2)}, u32[]{:S(2)}) async-start(f32[32,32,128]{2,1,0:T(8,128)} %get-tuple-element.11), calls=%async_computation.1 | async-start | bytes 1048576 | tf_op jit(solution)/shard_map/all_to_all | solution.py:434
  33.8 1.1 %surf_pack.1 = (f32[8,16,128]{2,1,0:T(8,128)S(1)}, f32[8,16,128]{2,1,0:T(8,128)S(1)}) custom-call(s32[1]{0:T(128)} %bitcast.3.me_ref, f32[12,512]{1,0:T(8,128)} %conc_ref.3, f32[1,512]{1,0:T(1,128)} %bitcast.11, s32[1,512]{1,0:T(1,128)} %bitcast.13, s32[1,512]{1,0:T(1,128)} %bitcast.15), custom_call_target="tpu_custom_call" | custom-call | tf_op jit(solution)/shard_map/surf_pack/pallas_call | solution.py:468
  35.0 7.4 %collective-permute-start = (f32[8,16,128]{2,1,0:T(8,128)S(1)}, f32[8,16,128]{2,1,0:T(8,128)S(1)}, u32[]{:S(2)}, u32[]{:S(2)}) collective-permute-start(f32[8,16,128]{2,1,0:T(8,128)S(1)} %get-tuple-element.13), channel_id=1, source_target_pairs={{0,256},{32,288},{64,320},{96,352},{128,384},{160,416},{192,448},{... | collective-permute-start | bytes 196616 | tf_op jit(solution)/shard_map/ppermute | solution.py:415
  42.4 1.9 %collective-permute-done = f32[8,16,128]{2,1,0:T(8,128)S(1)} collective-permute-done((f32[8,16,128]{2,1,0:T(8,128)S(1)}, f32[8,16,128]{2,1,0:T(8,128)S(1)}, u32[]{:S(2)}, u32[]{:S(2)}) %collective-permute-start) | collective-permute-done | bytes 65568 | tf_op jit(solution)/shard_map/ppermute | solution.py:415
  44.4 4.7 %collective-permute-start.1 = (f32[4,16,128]{2,1,0:T(8,128)S(1)}, f32[4,16,128]{2,1,0:T(8,128)S(1)}, u32[]{:S(2)}, u32[]{:S(2)}) collective-permute-start(f32[4,16,128]{2,1,0:T(8,128)S(1)} %slice_add_fusion), channel_id=1, source_target_pairs={{0,128},{32,160},{64,192},{96,224},{128,0},{160,32},{192,64},{224,... | collective-permute-start | bytes 98312 | tf_op jit(solution)/shard_map/ppermute | solution.py:415
  49.1 1.6 %collective-permute-done.1 = f32[4,16,128]{2,1,0:T(8,128)S(1)} collective-permute-done((f32[4,16,128]{2,1,0:T(8,128)S(1)}, f32[4,16,128]{2,1,0:T(8,128)S(1)}, u32[]{:S(2)}, u32[]{:S(2)}) %collective-permute-start.1) | collective-permute-done | bytes 32800 | tf_op jit(solution)/shard_map/ppermute | solution.py:415
  50.6 2.6 %collective-permute-start.2 = (f32[2,16,128]{2,1,0:T(8,128)S(1)}, f32[2,16,128]{2,1,0:T(8,128)S(1)}, u32[]{:S(2)}, u32[]{:S(2)}) collective-permute-start(f32[2,16,128]{2,1,0:T(8,128)S(1)} %slice_add_fusion.1), channel_id=1, source_target_pairs={{0,64},{32,96},{64,0},{96,32},{128,192},{160,224},{192,128},{224,1... | collective-permute-start | bytes 49160 | tf_op jit(solution)/shard_map/ppermute | solution.py:415
  53.2 1.9 %collective-permute-done.2 = f32[2,16,128]{2,1,0:T(8,128)S(1)} collective-permute-done((f32[2,16,128]{2,1,0:T(8,128)S(1)}, f32[2,16,128]{2,1,0:T(8,128)S(1)}, u32[]{:S(2)}, u32[]{:S(2)}) %collective-permute-start.2) | collective-permute-done | bytes 16416 | tf_op jit(solution)/shard_map/ppermute | solution.py:415
  55.1 6.5 %collective-permute-start.3 = (f32[1,16,128]{2,1,0:T(8,128)S(1)}, f32[1,16,128]{2,1,0:T(8,128)S(1)}, u32[]{:S(2)}, u32[]{:S(2)}) collective-permute-start(f32[1,16,128]{2,1,0:T(8,128)S(1)} %get-tuple-element.16), channel_id=1, source_target_pairs={{0,32},{32,0},{64,96},{96,64},{128,160},{160,128},{192,224},{224,1... | collective-permute-start | bytes 24584 | tf_op jit(solution)/shard_map/ppermute | solution.py:415
  61.8 0.6 collective-permute-done.3.refs_4_
  62.4 1.4 %interface.1 = (f32[768,128]{1,0:T(8,128)}, f32[1,16,128]{2,1,0:T(8,128)S(1)}) custom-call(f32[1024,128]{1,0:T(8,128)S(1)} %bitcast.10, s32[1,128]{1,0:T(1,128)S(1)} %bitcast.17, f32[1,16,128]{2,1,0:T(8,128)S(1)} %get-tuple-element.17.refs_0_, f32[1,16,128]{2,1,0:T(8,128)S(1)} %get-tuple-element.18.refs_1_, f32[1,16,128]{2,1,0:T(8,128)S(1)} %get-tuple-element.19.refs_2_, ...), custom_call_target="tpu_custom_call" | custom-call | tf_op jit(solution)/shard_map/interface/pallas_call | solution.py:430
  63.8 8.1 %collective-permute-start.4 = (f32[1,16,128]{2,1,0:T(8,128)S(1)}, f32[1,16,128]{2,1,0:T(8,128)S(1)}, u32[]{:S(2)}, u32[]{:S(2)}) collective-permute-start(f32[1,16,128]{2,1,0:T(8,128)S(1)} %get-tuple-element.15), channel_id=1, source_target_pairs={{0,256},{32,288},{64,320},{96,352},{128,384},{160,416},{192,448},{... | collective-permute-start | bytes 24584 | tf_op jit(solution)/shard_map/ppermute | solution.py:415
  72.0 9.4 %all-to-all-start.2 = ((f32[32,24,128]{2,1,0:T(8,128)}), f32[32,24,128]{2,1,0:T(8,128)S(1)}, u32[]{:S(2)}, u32[]{:S(2)}) async-start(f32[32,24,128]{2,1,0:T(8,128)} %bitcast.7), calls=%async_computation.2 | async-start | bytes 786432 | tf_op jit(solution)/shard_map/all_to_all | solution.py:434
  81.4 1.9 %collective-permute-start.5 = (f32[2,16,128]{2,1,0:T(8,128)S(1)}, f32[2,16,128]{2,1,0:T(8,128)S(1)}, u32[]{:S(2)}, u32[]{:S(2)}) collective-permute-start(f32[2,16,128]{2,1,0:T(8,128)S(1)} %pad_maximum_fusion.1), channel_id=1, source_target_pairs={{0,128},{32,160},{64,192},{96,224},{128,0},{160,32},{192,64},{224,... | collective-permute-start | bytes 49160 | tf_op jit(solution)/shard_map/ppermute | solution.py:415
  83.3 3.7 %collective-permute-done.5 = f32[2,16,128]{2,1,0:T(8,128)S(1)} collective-permute-done((f32[2,16,128]{2,1,0:T(8,128)S(1)}, f32[2,16,128]{2,1,0:T(8,128)S(1)}, u32[]{:S(2)}, u32[]{:S(2)}) %collective-permute-start.5) | collective-permute-done | bytes 16416 | tf_op jit(solution)/shard_map/ppermute | solution.py:415
  87.0 1.9 %collective-permute-start.6 = (f32[4,16,128]{2,1,0:T(8,128)S(1)}, f32[4,16,128]{2,1,0:T(8,128)S(1)}, u32[]{:S(2)}, u32[]{:S(2)}) collective-permute-start(f32[4,16,128]{2,1,0:T(8,128)S(1)} %pad_maximum_fusion), channel_id=1, source_target_pairs={{0,64},{32,96},{64,0},{96,32},{128,192},{160,224},{192,128},{224,1... | collective-permute-start | bytes 98312 | tf_op jit(solution)/shard_map/ppermute | solution.py:415
  89.0 3.0 %collective-permute-done.6 = f32[4,16,128]{2,1,0:T(8,128)S(1)} collective-permute-done((f32[4,16,128]{2,1,0:T(8,128)S(1)}, f32[4,16,128]{2,1,0:T(8,128)S(1)}, u32[]{:S(2)}, u32[]{:S(2)}) %collective-permute-start.6) | collective-permute-done | bytes 32800 | tf_op jit(solution)/shard_map/ppermute | solution.py:415
  92.0 4.5 %collective-permute-start.7 = (f32[8,16,128]{2,1,0:T(8,128)S(1)}, f32[8,16,128]{2,1,0:T(8,128)S(1)}, u32[]{:S(2)}, u32[]{:S(2)}) collective-permute-start(f32[8,16,128]{2,1,0:T(8,128)S(1)} %constant_dynamic-update-slice_fusion.near_ref), channel_id=1, source_target_pairs={{0,32},{32,0},{64,96},{96,64},{128,160},{160,128},{192,224},{224,1... | collective-permute-start | bytes 196616 | tf_op jit(solution)/shard_map/ppermute | solution.py:415
  97.4 1.0 surf_flux.1
  98.4 5.6 %speciate.1 = f32[12,8,4096]{2,1,0:T(8,128)} custom-call(f32[12,8,4096]{2,1,0:T(8,128)S(1)} %get-tuple-element.9.g_ref, f32[2,8,4096]{2,1,0:T(8,128)S(1)} %get-tuple-element.10.vw_ref, f32[8,4096]{1,0:T(8,128)S(1)} %copy-done, f32[32,24,128]{2,1,0:T(8,128)S(1)} %all-to-all-done.2.ends_ref, f32[32,16,128]{2,1,0:T(8,128)S(1)} %lookup.1.sorb_ref), custom_call_target="tpu_custom_call" | custom-call | tf_op jit(solution)/shard_map/speciate/pallas_call | solution.py:526
  (35 shorter events, 1.1 us)
Async XLA Ops:
  2.0 22.5 %all-to-all-start = ((s32[32,2,128]{2,1,0:T(2,128)}), s32[32,2,128]{2,1,0:T(2,128)S(1)}, u32[]{:S(2)}, u32[]{:S(2)}) async-start(s32[32,2,128]{2,1,0:T(2,128)} %broadcast_select_fusion), calls=%async_computation | async-start | bytes 65536 | tf_op jit(solution)/shard_map/all_to_all | solution.py:434
  24.5 37.1 %copy-start.6 = (f32[16,12]{1,0:T(8,128)S(1)}, f32[16,12]{1,0:T(8,128)}, u32[]{:S(2)}) copy-start(f32[16,12]{1,0:T(8,128)} %param.18) | copy-start | bytes 2308
  24.5 38.0 %copy-start.5 = (s32[128]{0:T(128)S(1)}, s32[128]{0:T(128)}, u32[]{:S(2)}) copy-start(s32[128]{0:T(128)} %param.16) | copy-start | bytes 1540
  29.7 66.8 %copy-start.7 = (f32[16]{0:T(128)S(1)}, f32[16]{0:T(128)}, u32[]{:S(2)}) copy-start(f32[16]{0:T(128)} %param.19) | copy-start | bytes 196
  29.7 67.7 %copy-start.1 = (f32[12,512]{1,0:T(8,128)S(1)}, f32[12,512]{1,0:T(8,128)}, u32[]{:S(2)}) copy-start(f32[12,512]{1,0:T(8,128)} %conc_ref.3) | copy-start | bytes 73732
  29.7 67.7 %copy-start.2 = (f32[512]{0:T(512)S(1)}, f32[512]{0:T(512)}, u32[]{:S(2)}) copy-start(f32[512]{0:T(512)} %param.21) | copy-start | bytes 6148
  29.7 67.7 %copy-start.3 = (s32[512,1]{0,1:T(1,128)S(1)}, s32[512,1]{0,1:T(1,128)}, u32[]{:S(2)}) copy-start(s32[512,1]{0,1:T(1,128)} %param.22) | copy-start | bytes 6148
  29.7 67.7 %copy-start.4 = (s32[512]{0:T(512)S(1)}, s32[512]{0:T(512)}, u32[]{:S(2)}) copy-start(s32[512]{0:T(512)} %param.23) | copy-start | bytes 6148
  29.8 68.6 %copy-start = (f32[8,4096]{1,0:T(8,128)S(1)}, f32[8,4096]{1,0:T(8,128)}, u32[]{:S(2)}) copy-start(f32[8,4096]{1,0:T(8,128)} %theta_ref.1) | copy-start | bytes 393220
  29.8 32.7 %all-to-all-start.1 = ((f32[32,32,128]{2,1,0:T(8,128)}), f32[32,32,128]{2,1,0:T(8,128)S(1)}, u32[]{:S(2)}, u32[]{:S(2)}) async-start(f32[32,32,128]{2,1,0:T(8,128)} %get-tuple-element.11), calls=%async_computation.1 | async-start | bytes 1048576 | tf_op jit(solution)/shard_map/all_to_all | solution.py:434
  35.0 9.4 %collective-permute-start = (f32[8,16,128]{2,1,0:T(8,128)S(1)}, f32[8,16,128]{2,1,0:T(8,128)S(1)}, u32[]{:S(2)}, u32[]{:S(2)}) collective-permute-start(f32[8,16,128]{2,1,0:T(8,128)S(1)} %get-tuple-element.13), channel_id=1, source_target_pairs={{0,256},{32,288},{64,320},{96,352},{128,384},{160,416},{192,448},{... | collective-permute-start | bytes 196616 | tf_op jit(solution)/shard_map/ppermute | solution.py:415
  44.4 6.3 %collective-permute-start.1 = (f32[4,16,128]{2,1,0:T(8,128)S(1)}, f32[4,16,128]{2,1,0:T(8,128)S(1)}, u32[]{:S(2)}, u32[]{:S(2)}) collective-permute-start(f32[4,16,128]{2,1,0:T(8,128)S(1)} %slice_add_fusion), channel_id=1, source_target_pairs={{0,128},{32,160},{64,192},{96,224},{128,0},{160,32},{192,64},{224,... | collective-permute-start | bytes 98312 | tf_op jit(solution)/shard_map/ppermute | solution.py:415
  50.6 4.5 %collective-permute-start.2 = (f32[2,16,128]{2,1,0:T(8,128)S(1)}, f32[2,16,128]{2,1,0:T(8,128)S(1)}, u32[]{:S(2)}, u32[]{:S(2)}) collective-permute-start(f32[2,16,128]{2,1,0:T(8,128)S(1)} %slice_add_fusion.1), channel_id=1, source_target_pairs={{0,64},{32,96},{64,0},{96,32},{128,192},{160,224},{192,128},{224,1... | collective-permute-start | bytes 49160 | tf_op jit(solution)/shard_map/ppermute | solution.py:415
  55.1 7.3 %collective-permute-start.3 = (f32[1,16,128]{2,1,0:T(8,128)S(1)}, f32[1,16,128]{2,1,0:T(8,128)S(1)}, u32[]{:S(2)}, u32[]{:S(2)}) collective-permute-start(f32[1,16,128]{2,1,0:T(8,128)S(1)} %get-tuple-element.16), channel_id=1, source_target_pairs={{0,32},{32,0},{64,96},{96,64},{128,160},{160,128},{192,224},{224,1... | collective-permute-start | bytes 24584 | tf_op jit(solution)/shard_map/ppermute | solution.py:415
  63.8 17.5 %collective-permute-start.4 = (f32[1,16,128]{2,1,0:T(8,128)S(1)}, f32[1,16,128]{2,1,0:T(8,128)S(1)}, u32[]{:S(2)}, u32[]{:S(2)}) collective-permute-start(f32[1,16,128]{2,1,0:T(8,128)S(1)} %get-tuple-element.15), channel_id=1, source_target_pairs={{0,256},{32,288},{64,320},{96,352},{128,384},{160,416},{192,448},{... | collective-permute-start | bytes 24584 | tf_op jit(solution)/shard_map/ppermute | solution.py:415
  72.0 26.4 %all-to-all-start.2 = ((f32[32,24,128]{2,1,0:T(8,128)}), f32[32,24,128]{2,1,0:T(8,128)S(1)}, u32[]{:S(2)}, u32[]{:S(2)}) async-start(f32[32,24,128]{2,1,0:T(8,128)} %bitcast.7), calls=%async_computation.2 | async-start | bytes 786432 | tf_op jit(solution)/shard_map/all_to_all | solution.py:434
  81.4 5.7 %collective-permute-start.5 = (f32[2,16,128]{2,1,0:T(8,128)S(1)}, f32[2,16,128]{2,1,0:T(8,128)S(1)}, u32[]{:S(2)}, u32[]{:S(2)}) collective-permute-start(f32[2,16,128]{2,1,0:T(8,128)S(1)} %pad_maximum_fusion.1), channel_id=1, source_target_pairs={{0,128},{32,160},{64,192},{96,224},{128,0},{160,32},{192,64},{224,... | collective-permute-start | bytes 49160 | tf_op jit(solution)/shard_map/ppermute | solution.py:415
  87.0 4.9 %collective-permute-start.6 = (f32[4,16,128]{2,1,0:T(8,128)S(1)}, f32[4,16,128]{2,1,0:T(8,128)S(1)}, u32[]{:S(2)}, u32[]{:S(2)}) collective-permute-start(f32[4,16,128]{2,1,0:T(8,128)S(1)} %pad_maximum_fusion), channel_id=1, source_target_pairs={{0,64},{32,96},{64,0},{96,32},{128,192},{160,224},{192,128},{224,1... | collective-permute-start | bytes 98312 | tf_op jit(solution)/shard_map/ppermute | solution.py:415
  92.0 5.4 %collective-permute-start.7 = (f32[8,16,128]{2,1,0:T(8,128)S(1)}, f32[8,16,128]{2,1,0:T(8,128)S(1)}, u32[]{:S(2)}, u32[]{:S(2)}) collective-permute-start(f32[8,16,128]{2,1,0:T(8,128)S(1)} %constant_dynamic-update-slice_fusion.near_ref), channel_id=1, source_target_pairs={{0,32},{32,0},{64,96},{96,64},{128,160},{160,128},{192,224},{224,1... | collective-permute-start | bytes 196616 | tf_op jit(solution)/shard_map/ppermute | solution.py:415

commit v3 on v2

--- a/solution.py
+++ b/solution.py
@@ -21,6 +21,12 @@
 
 def rows_iota(shape):
     return lax.broadcasted_iota(jnp.int32, shape, 0)
+
+
+def meta_kernel(class_ref, active_ref, out_ref):
+    both = jnp.concatenate([class_ref[...], active_ref[...]], axis=0)
+    for t in range(out_ref.shape[0]):
+        out_ref[t] = both
 
 
 def surf_pack_kernel(
@@ -78,8 +84,13 @@
     return masks
 
 
+def doublings(n):
+    masks = halvings(n)
+    return [masks[k] for k in (0, 3, 2, 1) if k < len(masks)]
+
+
 def slot_mask(i, n):
-    return sum(m for k, m in enumerate(halvings(n)) if i >> k & 1)
+    return sum(m for k, m in enumerate(doublings(n)) if i >> k & 1)
 
 
 def eliminate_kernel(
@@ -388,7 +399,7 @@
 
 
 PAIR = 2
-CHUNKS = 4
+CHUNKS = 8
 
 
 VMEM, HBM = pltpu.VMEM, pltpu.HBM
@@ -455,8 +466,15 @@
     sds = jax.ShapeDtypeStruct
     first = (lax.axis_index("col") * depth).astype(jnp.int32).reshape(1)
 
-    kind = lax.broadcasted_iota(jnp.int32, (owners, 2, LANES), 1)
-    meta = jnp.where(kind == 0, soil_class[None, None], active[None, None])
+    meta = pl.pallas_call(
+        meta_kernel,
+        out_shape=sds((owners, 2, LANES), jnp.int32),
+        in_specs=[full()] * 2,
+        out_specs=full(),
+        interpret=INTERPRET,
+        compiler_params=pltpu.CompilerParams(vmem_limit_bytes=24 << 20),
+        name="meta",
+    )(far(soil_class.reshape(1, LANES)), far(active.reshape(1, LANES)))
     meta = exchange(meta, "col")
 
     rate = surf_rate.reshape(1, n)
@@ -518,7 +536,7 @@
         name="interface",
     )(recv.reshape(owners * 32, LANES), active.reshape(1, LANES), *surf_parts)
     ends = exchange(ends.reshape(owners, 24, LANES), "col")
-    for k, mask in enumerate(masks):
+    for k, mask in enumerate(doublings(groups)):
         if k:
             top = jnp.concatenate([top, other], axis=0)
         other = swap(top, mask)

time: 105 us -> 105 us (level)
  the two profiles are of different devices: /device:TPU:1 before, /device:TPU:2 now
where the time goes in v3:
time: 105 us; the launch traced here: 104 us
  starting transfers between devices  60.8 us (58%)
  waiting for transfers between devices  25.9 us (25%)
  Pallas kernels  16 us (15%)
    ppermute x8, starting transfers between devices, swap(): return lax.ppermute(x, 'grp', [(i, i ^ mask) for i in range(n)])  32.3 us
    all_to_all x3, starting transfers between devices, exchange(): return lax.all_to_all(x, axis, split_axis=0, concat_axis=0, tiled=True)  28.5 us
    ppermute x8, waiting for transfers between devices, swap(): return lax.ppermute(x, 'grp', [(i, i ^ mask) for i in range(n)])  17.2 us
    all_to_all x3, waiting for transfers between devices, exchange(): return lax.all_to_all(x, axis, split_axis=0, concat_axis=0, tiled=True)  8.68 us
    pallas_call x1, Pallas kernels, step(): pl.pallas_call(speciate_kernel, out_shape=sds((comps, depth, width), F32)...  5.6 us
    pallas_call x1, Pallas kernels, step(): pl.pallas_call(eliminate_kernel, out_shape=(held((owners, 32, LANES)), he...  5.25 us
  transfers between devices with their start and end apart: 11, of which 8 were waited for; matrix products, arithmetic and copies ran while one was open for 0% of the time, Pallas kernels for 2%

profile of v3, /device:TPU:2, one launch (start us, length us, event | category | flops | bytes accessed | tf_op | source)
XLA Modules:
  0.0 103.9 jit_solution(9735054845219380757)
XLA Ops:
  0.6 1.3 %meta.1 = s32[32,2,128]{2,1,0:T(2,128)} custom-call(s32[1,128]{1,0:T(1,128)} %bitcast.21, s32[1,128]{1,0:T(1,128)} %bitcast.18), custom_call_target="tpu_custom_call" | custom-call | tf_op jit(solution)/shard_map/meta/pallas_call | solution.py:469
  1.9 13.5 %all-to-all-start = ((s32[32,2,128]{2,1,0:T(2,128)}), s32[32,2,128]{2,1,0:T(2,128)S(1)}, u32[]{:S(2)}, u32[]{:S(2)}) async-start(s32[32,2,128]{2,1,0:T(2,128)} %meta.1), calls=%async_computation | async-start | bytes 65536 | tf_op jit(solution)/shard_map/all_to_all | solution.py:445
  15.4 8.7 %all-to-all-done.meta_ref = s32[32,2,128]{2,1,0:T(2,128)S(1)} async-done(((s32[32,2,128]{2,1,0:T(2,128)}), s32[32,2,128]{2,1,0:T(2,128)S(1)}, u32[]{:S(2)}, u32[]{:S(2)}) %all-to-all-start) | async-done | bytes 32800 | tf_op jit(solution)/shard_map/all_to_all | solution.py:445
  24.1 5.3 %eliminate.1 = (f32[32,32,128]{2,1,0:T(8,128)}, f32[12,8,4096]{2,1,0:T(8,128)S(1)}, f32[2,8,4096]{2,1,0:T(8,128)S(1)}) custom-call(s32[1]{0:T(128)} %bitcast.first_ref, f32[16]{0:T(128)} %table_ref.1, f32[12,8,4096]{2,1,0:T(8,128)} %conc_hbm.1, f32[8,4096]{1,0:T(8,128)} %theta_ref.1, f32[8,4096]{1,0:T(8,128)} %cond_hbm.1, ...), custom_call_target="tpu_custom_call" | custom-call | tf_op jit(solution)/shard_map/eliminate/pallas_call | solution.py:506
  29.4 5.2 %all-to-all-start.1 = ((f32[32,32,128]{2,1,0:T(8,128)}), f32[32,32,128]{2,1,0:T(8,128)S(1)}, u32[]{:S(2)}, u32[]{:S(2)}) async-start(f32[32,32,128]{2,1,0:T(8,128)} %get-tuple-element.11), calls=%async_computation.1 | async-start | bytes 1048576 | tf_op jit(solution)/shard_map/all_to_all | solution.py:445
  34.6 1.1 %surf_pack.1 = (f32[8,16,128]{2,1,0:T(8,128)S(1)}, f32[8,16,128]{2,1,0:T(8,128)S(1)}) custom-call(s32[1]{0:T(128)} %bitcast.4.me_ref, f32[12,512]{1,0:T(8,128)} %conc_ref.3, f32[1,512]{1,0:T(1,128)} %bitcast.12, s32[1,512]{1,0:T(1,128)} %bitcast.14, s32[1,512]{1,0:T(1,128)} %bitcast.16), custom_call_target="tpu_custom_call" | custom-call | tf_op jit(solution)/shard_map/surf_pack/pallas_call | solution.py:486
  35.8 7.7 %collective-permute-start = (f32[8,16,128]{2,1,0:T(8,128)S(1)}, f32[8,16,128]{2,1,0:T(8,128)S(1)}, u32[]{:S(2)}, u32[]{:S(2)}) collective-permute-start(f32[8,16,128]{2,1,0:T(8,128)S(1)} %get-tuple-element.13), channel_id=1, source_target_pairs={{0,256},{32,288},{64,320},{96,352},{128,384},{160,416},{192,448},{... | collective-permute-start | bytes 196616 | tf_op jit(solution)/shard_map/ppermute | solution.py:426
  43.5 2.5 %collective-permute-done = f32[8,16,128]{2,1,0:T(8,128)S(1)} collective-permute-done((f32[8,16,128]{2,1,0:T(8,128)S(1)}, f32[8,16,128]{2,1,0:T(8,128)S(1)}, u32[]{:S(2)}, u32[]{:S(2)}) %collective-permute-start) | collective-permute-done | bytes 65568 | tf_op jit(solution)/shard_map/ppermute | solution.py:426
  46.0 4.9 %collective-permute-start.1 = (f32[4,16,128]{2,1,0:T(8,128)S(1)}, f32[4,16,128]{2,1,0:T(8,128)S(1)}, u32[]{:S(2)}, u32[]{:S(2)}) collective-permute-start(f32[4,16,128]{2,1,0:T(8,128)S(1)} %slice_add_fusion), channel_id=1, source_target_pairs={{0,128},{32,160},{64,192},{96,224},{128,0},{160,32},{192,64},{224,... | collective-permute-start | bytes 98312 | tf_op jit(solution)/shard_map/ppermute | solution.py:426
  50.9 1.9 %collective-permute-done.1 = f32[4,16,128]{2,1,0:T(8,128)S(1)} collective-permute-done((f32[4,16,128]{2,1,0:T(8,128)S(1)}, f32[4,16,128]{2,1,0:T(8,128)S(1)}, u32[]{:S(2)}, u32[]{:S(2)}) %collective-permute-start.1) | collective-permute-done | bytes 32800 | tf_op jit(solution)/shard_map/ppermute | solution.py:426
  52.8 3.3 %collective-permute-start.2 = (f32[2,16,128]{2,1,0:T(8,128)S(1)}, f32[2,16,128]{2,1,0:T(8,128)S(1)}, u32[]{:S(2)}, u32[]{:S(2)}) collective-permute-start(f32[2,16,128]{2,1,0:T(8,128)S(1)} %slice_add_fusion.1), channel_id=1, source_target_pairs={{0,64},{32,96},{64,0},{96,32},{128,192},{160,224},{192,128},{224,1... | collective-permute-start | bytes 49160 | tf_op jit(solution)/shard_map/ppermute | solution.py:426
  56.2 2.3 %collective-permute-done.2 = f32[2,16,128]{2,1,0:T(8,128)S(1)} collective-permute-done((f32[2,16,128]{2,1,0:T(8,128)S(1)}, f32[2,16,128]{2,1,0:T(8,128)S(1)}, u32[]{:S(2)}, u32[]{:S(2)}) %collective-permute-start.2) | collective-permute-done | bytes 16416 | tf_op jit(solution)/shard_map/ppermute | solution.py:426
  58.5 1.9 %collective-permute-start.3 = (f32[1,16,128]{2,1,0:T(8,128)S(1)}, f32[1,16,128]{2,1,0:T(8,128)S(1)}, u32[]{:S(2)}, u32[]{:S(2)}) collective-permute-start(f32[1,16,128]{2,1,0:T(8,128)S(1)} %get-tuple-element.16), channel_id=1, source_target_pairs={{0,32},{32,0},{64,96},{96,64},{128,160},{160,128},{192,224},{224,1... | collective-permute-start | bytes 24584 | tf_op jit(solution)/shard_map/ppermute | solution.py:426
  61.5 1.4 %interface.1 = (f32[768,128]{1,0:T(8,128)}, f32[1,16,128]{2,1,0:T(8,128)S(1)}) custom-call(f32[1024,128]{1,0:T(8,128)S(1)} %bitcast.11, s32[1,128]{1,0:T(1,128)S(1)} %bitcast.19, f32[1,16,128]{2,1,0:T(8,128)S(1)} %get-tuple-element.17.refs_0_, f32[1,16,128]{2,1,0:T(8,128)S(1)} %get-tuple-element.18.refs_1_, f32[1,16,128]{2,1,0:T(8,128)S(1)} %get-tuple-element.19.refs_2_, ...), custom_call_target="tpu_custom_call" | custom-call | tf_op jit(solution)/shard_map/interface/pallas_call | solution.py:441
  62.9 8.2 %collective-permute-start.4 = (f32[1,16,128]{2,1,0:T(8,128)S(1)}, f32[1,16,128]{2,1,0:T(8,128)S(1)}, u32[]{:S(2)}, u32[]{:S(2)}) collective-permute-start(f32[1,16,128]{2,1,0:T(8,128)S(1)} %get-tuple-element.15), channel_id=1, source_target_pairs={{0,256},{32,288},{64,320},{96,352},{128,384},{160,416},{192,448},{... | collective-permute-start | bytes 24584 | tf_op jit(solution)/shard_map/ppermute | solution.py:426
  71.2 9.9 %all-to-all-start.2 = ((f32[32,24,128]{2,1,0:T(8,128)}), f32[32,24,128]{2,1,0:T(8,128)S(1)}, u32[]{:S(2)}, u32[]{:S(2)}) async-start(f32[32,24,128]{2,1,0:T(8,128)} %bitcast.8), calls=%async_computation.2 | async-start | bytes 786432 | tf_op jit(solution)/shard_map/all_to_all | solution.py:445
  81.0 1.9 %collective-permute-start.5 = (f32[2,16,128]{2,1,0:T(8,128)S(1)}, f32[2,16,128]{2,1,0:T(8,128)S(1)}, u32[]{:S(2)}, u32[]{:S(2)}) collective-permute-start(f32[2,16,128]{2,1,0:T(8,128)S(1)} %pad_maximum_fusion.1), channel_id=1, source_target_pairs={{0,32},{32,0},{64,96},{96,64},{128,160},{160,128},{192,224},{224,1... | collective-permute-start | bytes 49160 | tf_op jit(solution)/shard_map/ppermute | solution.py:426
  83.0 1.1 %collective-permute-done.5 = f32[2,16,128]{2,1,0:T(8,128)S(1)} collective-permute-done((f32[2,16,128]{2,1,0:T(8,128)S(1)}, f32[2,16,128]{2,1,0:T(8,128)S(1)}, u32[]{:S(2)}, u32[]{:S(2)}) %collective-permute-start.5) | collective-permute-done | bytes 16416 | tf_op jit(solution)/shard_map/ppermute | solution.py:426
  84.1 2.1 %collective-permute-start.6 = (f32[4,16,128]{2,1,0:T(8,128)S(1)}, f32[4,16,128]{2,1,0:T(8,128)S(1)}, u32[]{:S(2)}, u32[]{:S(2)}) collective-permute-start(f32[4,16,128]{2,1,0:T(8,128)S(1)} %pad_maximum_fusion), channel_id=1, source_target_pairs={{0,64},{32,96},{64,0},{96,32},{128,192},{160,224},{192,128},{224,1... | collective-permute-start | bytes 98312 | tf_op jit(solution)/shard_map/ppermute | solution.py:426
  86.3 3.7 %collective-permute-done.6 = f32[4,16,128]{2,1,0:T(8,128)S(1)} collective-permute-done((f32[4,16,128]{2,1,0:T(8,128)S(1)}, f32[4,16,128]{2,1,0:T(8,128)S(1)}, u32[]{:S(2)}, u32[]{:S(2)}) %collective-permute-start.6) | collective-permute-done | bytes 32800 | tf_op jit(solution)/shard_map/ppermute | solution.py:426
  89.9 2.1 %collective-permute-start.7 = (f32[8,16,128]{2,1,0:T(8,128)S(1)}, f32[8,16,128]{2,1,0:T(8,128)S(1)}, u32[]{:S(2)}, u32[]{:S(2)}) collective-permute-start(f32[8,16,128]{2,1,0:T(8,128)S(1)} %constant_dynamic-update-slice_fusion.near_ref), channel_id=1, source_target_pairs={{0,128},{32,160},{64,192},{96,224},{128,0},{160,32},{192,64},{224,... | collective-permute-start | bytes 196616 | tf_op jit(solution)/shard_map/ppermute | solution.py:426
  92.5 4.8 %collective-permute-done.7.far_ref = f32[8,16,128]{2,1,0:T(8,128)S(1)} collective-permute-done((f32[8,16,128]{2,1,0:T(8,128)S(1)}, f32[8,16,128]{2,1,0:T(8,128)S(1)}, u32[]{:S(2)}, u32[]{:S(2)}) %collective-permute-start.7) | collective-permute-done | bytes 65568 | tf_op jit(solution)/shard_map/ppermute | solution.py:426
  97.4 1.0 surf_flux.1
  98.3 5.6 %speciate.1 = f32[12,8,4096]{2,1,0:T(8,128)} custom-call(f32[12,8,4096]{2,1,0:T(8,128)S(1)} %get-tuple-element.9.g_ref, f32[2,8,4096]{2,1,0:T(8,128)S(1)} %get-tuple-element.10.vw_ref, f32[8,4096]{1,0:T(8,128)S(1)} %copy-done, f32[32,24,128]{2,1,0:T(8,128)S(1)} %all-to-all-done.2.ends_ref, f32[32,16,128]{2,1,0:T(8,128)S(1)} %lookup.1.sorb_ref), custom_call_target="tpu_custom_call" | custom-call | tf_op jit(solution)/shard_map/speciate/pallas_call | solution.py:544
  (34 shorter events, 1.7 us)
Async XLA Ops:
  1.9 22.1 %all-to-all-start = ((s32[32,2,128]{2,1,0:T(2,128)}), s32[32,2,128]{2,1,0:T(2,128)S(1)}, u32[]{:S(2)}, u32[]{:S(2)}) async-start(s32[32,2,128]{2,1,0:T(2,128)} %meta.1), calls=%async_computation | async-start | bytes 65536 | tf_op jit(solution)/shard_map/all_to_all | solution.py:445
  24.1 36.3 %copy-start.6 = (f32[16,12]{1,0:T(8,128)S(1)}, f32[16,12]{1,0:T(8,128)}, u32[]{:S(2)}) copy-start(f32[16,12]{1,0:T(8,128)} %param.18) | copy-start | bytes 2308
  24.1 37.4 %copy-start.5 = (s32[128]{0:T(128)S(1)}, s32[128]{0:T(128)}, u32[]{:S(2)}) copy-start(s32[128]{0:T(128)} %param.16) | copy-start | bytes 1540
  29.3 62.7 %copy-start.7 = (f32[16]{0:T(128)S(1)}, f32[16]{0:T(128)}, u32[]{:S(2)}) copy-start(f32[16]{0:T(128)} %param.19) | copy-start | bytes 196
  29.4 68.0 %copy-start.1 = (f32[12,512]{1,0:T(8,128)S(1)}, f32[12,512]{1,0:T(8,128)}, u32[]{:S(2)}) copy-start(f32[12,512]{1,0:T(8,128)} %conc_ref.3) | copy-start | bytes 73732
  29.4 68.0 %copy-start.2 = (f32[512]{0:T(512)S(1)}, f32[512]{0:T(512)}, u32[]{:S(2)}) copy-start(f32[512]{0:T(512)} %param.21) | copy-start | bytes 6148
  29.4 68.0 %copy-start.3 = (s32[512,1]{0,1:T(1,128)S(1)}, s32[512,1]{0,1:T(1,128)}, u32[]{:S(2)}) copy-start(s32[512,1]{0,1:T(1,128)} %param.22) | copy-start | bytes 6148
  29.4 68.0 %copy-start.4 = (s32[512]{0:T(512)S(1)}, s32[512]{0:T(512)}, u32[]{:S(2)}) copy-start(s32[512]{0:T(512)} %param.23) | copy-start | bytes 6148
  29.4 68.9 %copy-start = (f32[8,4096]{1,0:T(8,128)S(1)}, f32[8,4096]{1,0:T(8,128)}, u32[]{:S(2)}) copy-start(f32[8,4096]{1,0:T(8,128)} %theta_ref.1) | copy-start | bytes 393220
  29.4 32.1 %all-to-all-start.1 = ((f32[32,32,128]{2,1,0:T(8,128)}), f32[32,32,128]{2,1,0:T(8,128)S(1)}, u32[]{:S(2)}, u32[]{:S(2)}) async-start(f32[32,32,128]{2,1,0:T(8,128)} %get-tuple-element.11), calls=%async_computation.1 | async-start | bytes 1048576 | tf_op jit(solution)/shard_map/all_to_all | solution.py:445
  35.8 10.2 %collective-permute-start = (f32[8,16,128]{2,1,0:T(8,128)S(1)}, f32[8,16,128]{2,1,0:T(8,128)S(1)}, u32[]{:S(2)}, u32[]{:S(2)}) collective-permute-start(f32[8,16,128]{2,1,0:T(8,128)S(1)} %get-tuple-element.13), channel_id=1, source_target_pairs={{0,256},{32,288},{64,320},{96,352},{128,384},{160,416},{192,448},{... | collective-permute-start | bytes 196616 | tf_op jit(solution)/shard_map/ppermute | solution.py:426
  46.0 6.8 %collective-permute-start.1 = (f32[4,16,128]{2,1,0:T(8,128)S(1)}, f32[4,16,128]{2,1,0:T(8,128)S(1)}, u32[]{:S(2)}, u32[]{:S(2)}) collective-permute-start(f32[4,16,128]{2,1,0:T(8,128)S(1)} %slice_add_fusion), channel_id=1, source_target_pairs={{0,128},{32,160},{64,192},{96,224},{128,0},{160,32},{192,64},{224,... | collective-permute-start | bytes 98312 | tf_op jit(solution)/shard_map/ppermute | solution.py:426
  52.8 5.6 %collective-permute-start.2 = (f32[2,16,128]{2,1,0:T(8,128)S(1)}, f32[2,16,128]{2,1,0:T(8,128)S(1)}, u32[]{:S(2)}, u32[]{:S(2)}) collective-permute-start(f32[2,16,128]{2,1,0:T(8,128)S(1)} %slice_add_fusion.1), channel_id=1, source_target_pairs={{0,64},{32,96},{64,0},{96,32},{128,192},{160,224},{192,128},{224,1... | collective-permute-start | bytes 49160 | tf_op jit(solution)/shard_map/ppermute | solution.py:426
  58.5 3.1 %collective-permute-start.3 = (f32[1,16,128]{2,1,0:T(8,128)S(1)}, f32[1,16,128]{2,1,0:T(8,128)S(1)}, u32[]{:S(2)}, u32[]{:S(2)}) collective-permute-start(f32[1,16,128]{2,1,0:T(8,128)S(1)} %get-tuple-element.16), channel_id=1, source_target_pairs={{0,32},{32,0},{64,96},{96,64},{128,160},{160,128},{192,224},{224,1... | collective-permute-start | bytes 24584 | tf_op jit(solution)/shard_map/ppermute | solution.py:426
  62.9 18.1 %collective-permute-start.4 = (f32[1,16,128]{2,1,0:T(8,128)S(1)}, f32[1,16,128]{2,1,0:T(8,128)S(1)}, u32[]{:S(2)}, u32[]{:S(2)}) collective-permute-start(f32[1,16,128]{2,1,0:T(8,128)S(1)} %get-tuple-element.15), channel_id=1, source_target_pairs={{0,256},{32,288},{64,320},{96,352},{128,384},{160,416},{192,448},{... | collective-permute-start | bytes 24584 | tf_op jit(solution)/shard_map/ppermute | solution.py:426
  71.2 27.2 %all-to-all-start.2 = ((f32[32,24,128]{2,1,0:T(8,128)}), f32[32,24,128]{2,1,0:T(8,128)S(1)}, u32[]{:S(2)}, u32[]{:S(2)}) async-start(f32[32,24,128]{2,1,0:T(8,128)} %bitcast.8), calls=%async_computation.2 | async-start | bytes 786432 | tf_op jit(solution)/shard_map/all_to_all | solution.py:445
  81.0 3.1 %collective-permute-start.5 = (f32[2,16,128]{2,1,0:T(8,128)S(1)}, f32[2,16,128]{2,1,0:T(8,128)S(1)}, u32[]{:S(2)}, u32[]{:S(2)}) collective-permute-start(f32[2,16,128]{2,1,0:T(8,128)S(1)} %pad_maximum_fusion.1), channel_id=1, source_target_pairs={{0,32},{32,0},{64,96},{96,64},{128,160},{160,128},{192,224},{224,1... | collective-permute-start | bytes 49160 | tf_op jit(solution)/shard_map/ppermute | solution.py:426
  84.1 5.8 %collective-permute-start.6 = (f32[4,16,128]{2,1,0:T(8,128)S(1)}, f32[4,16,128]{2,1,0:T(8,128)S(1)}, u32[]{:S(2)}, u32[]{:S(2)}) collective-permute-start(f32[4,16,128]{2,1,0:T(8,128)S(1)} %pad_maximum_fusion), channel_id=1, source_target_pairs={{0,64},{32,96},{64,0},{96,32},{128,192},{160,224},{192,128},{224,1... | collective-permute-start | bytes 98312 | tf_op jit(solution)/shard_map/ppermute | solution.py:426
  89.9 7.4 %collective-permute-start.7 = (f32[8,16,128]{2,1,0:T(8,128)S(1)}, f32[8,16,128]{2,1,0:T(8,128)S(1)}, u32[]{:S(2)}, u32[]{:S(2)}) collective-permute-start(f32[8,16,128]{2,1,0:T(8,128)S(1)} %constant_dynamic-update-slice_fusion.near_ref), channel_id=1, source_target_pairs={{0,128},{32,160},{64,192},{96,224},{128,0},{160,32},{192,64},{224,... | collective-permute-start | bytes 196616 | tf_op jit(solution)/shard_map/ppermute | solution.py:426

commit v4 on v3

--- a/solution.py
+++ b/solution.py
@@ -128,7 +128,7 @@
     for n in range(CHUNKS):
         for copy in in_copies(n):
             copy.start()
-    tiles = send_ref.shape[0]
+    tiles = send_ref.shape[0] // ROWS
     shape = (8, LANES)
     row = rows_iota(shape)
     zero = jnp.zeros(shape, F32)
@@ -150,11 +150,10 @@
         link = 2.0 * scaled * below / (scaled + below)
         link = jnp.where((row < 7) & (layer + 1 < active), link, zero)
         link_up = roll(link, 1)
-        up = jnp.where((row >= 2) & (row <= 6), link_up, zero)
-        dn = jnp.where((row >= 1) & (row <= 5), link, zero)
+        up = jnp.where(row >= 2, link_up, zero)
+        dn = jnp.where(row <= 5, link, zero)
         r_v = jnp.where(row == 1, link_up, zero)
         r_w = jnp.where(row == 6, link, zero)
-        r_e = jnp.where((row >= 1) & (row <= 6), theta, zero)
         excess = theta + r_v + r_w
         w1 = 1.0 / (excess + up + dn)
         t1 = excess * w1
@@ -170,7 +169,8 @@
         far = up3 + dn3
         w3 = 1.0 / (excess + far)
         excess = excess + far * roll(excess * w3, 4)
-        w4 = 1.0 / excess
+        inner = (row >= 1) & (row <= 6)
+        w4 = jnp.where(inner, 1.0 / excess, 1.0)
 
         def solve(r):
             q = r * w1
@@ -180,42 +180,24 @@
             r = r + far * roll(r * w3, 4)
             return r * w4
 
-        ends = jnp.where(row == 0, link, zero) + jnp.where(row == 7, link_up, zero)
-
-        def onto_ends(own, inner):
-            near = jnp.where(row == 0, roll(inner, -1), roll(inner, 1))
-            return own + ends * near
+        def put(r, value, layer):
+            send_ref[pl.ds(t * ROWS + r, 1), :] = value[layer : layer + 1]
 
         v = solve(r_v)
         w = solve(r_w)
-        e = solve(r_e)
-        vw_ref[0, :, cols] = jnp.where(row == 0, 1.0, v)
-        vw_ref[1, :, cols] = jnp.where(row == 7, 1.0, w)
-        diag = onto_ends(theta, e)
-        cross = onto_ends(zero, w)
-        mat = jnp.where(row == 0, diag, zero)
-        mat = jnp.where(row == 1, roll(diag, 2), mat)
-        mat = jnp.where(row == 2, roll(cross, 2), mat)
-        mat = jnp.where(row == 3, roll(scaled, 3), mat)
-        mat = jnp.where(row == 4, roll(scaled, 5), mat)
-        send_ref[t, 24:32, :] = mat
-        firsts, lasts, mixed = zero, zero, zero
+        e = solve(theta)
+        vw_ref[0, :, cols] = jnp.where(row == 0, 1.0, jnp.where(inner, v, zero))
+        vw_ref[1, :, cols] = jnp.where(row == 7, 1.0, jnp.where(inner, w, zero))
+        put(24, e, 0)
+        put(25, e, 7)
+        put(26, w, 0)
+        put(27, scaled, 0)
+        put(28, scaled, 7)
         for j in range(comps):
-            c = conc_ref[j, :, cols]
-            g = solve(r_e * c)
-            g_ref[j, :, cols] = g
-            z = onto_ends(theta * c, g)
-            if j < 8:
-                z = roll(z, j) if j else z
-                firsts = jnp.where(row == j, z, firsts)
-                lasts = jnp.where(row == (j + 7) % 8, z, lasts)
-            else:
-                k = j - 8
-                mixed = jnp.where(row == k, roll(z, k) if k else z, mixed)
-                mixed = jnp.where(row == k + 4, roll(z, k + 5), mixed)
-        send_ref[t, 0:8, :] = firsts
-        send_ref[t, 8:16, :] = lasts
-        send_ref[t, 16:24, :] = mixed
+            x = solve(theta * conc_ref[j, :, cols])
+            g_ref[j, :, cols] = jnp.where(inner, x, zero)
+            put(j, x, 0)
+            put(12 + j, x, 7)
 
     def tiles_of(i, carry):
         for k in range(FEW):
@@ -234,14 +216,7 @@
 
 
 FEW = 4
-
-
-def first_row(j):
-    return j if j < 8 else 16 + j - 8
-
-
-def last_row(j):
-    return 8 + (j + 7) % 8 if j < 8 else 20 + j - 8
+ROWS = 29
 
 
 def interface_kernel(recv_ref, active_ref, *refs):
@@ -256,7 +231,7 @@
         return pltpu.roll(v, d % blocks, 0)
 
     def take(r):
-        return recv_ref[pl.ds(r, blocks, stride=32), :]
+        return recv_ref[pl.ds(r, blocks, stride=ROWS), :]
 
     partial = tree_sum([ref[0] for ref in surf_refs])
     alpha = take(24) + jnp.where(row == 0, partial[comps : comps + 1], zero)
@@ -282,8 +257,8 @@
     w_end = 1.0 / excess
     tops = []
     for j in range(comps):
-        b = take(first_row(j)) + jnp.where(row == 0, partial[j : j + 1], zero)
-        r = take(last_row(j)) + cross_w * b + roll(link_w * b, -1)
+        b = take(j) + jnp.where(row == 0, partial[j : j + 1], zero)
+        r = take(12 + j) + cross_w * b + roll(link_w * b, -1)
         for d, up, dn, w in steps:
             q = r * w
             r = r + up * roll(q, d) + dn * roll(q, -d)
@@ -506,7 +481,7 @@
     send, g, vw = pl.pallas_call(
         eliminate_kernel,
         out_shape=(
-            held((owners, 32, LANES)),
+            held((owners * ROWS, LANES)),
             held((comps, depth, width)),
             held((2, depth, width)),
         ),
@@ -522,7 +497,7 @@
         compiler_params=pltpu.CompilerParams(vmem_limit_bytes=24 << 20),
         name="eliminate",
     )(first, far(class_cond), far(conc), far(porosity), far(cell_cond), near(meta))
-    recv = exchange(send, "col")
+    recv = exchange(send.reshape(owners, ROWS, 1, LANES), "col")
 
     table = jnp.concatenate(
         [sorb_affinity.T, sorb_capacity[None], jnp.zeros((15 - comps, 16), F32)], axis=0
@@ -534,7 +509,7 @@
         (held((owners * 24, LANES)), held((1, 16, LANES))),
         2 + len(surf_parts),
         name="interface",
-    )(recv.reshape(owners * 32, LANES), active.reshape(1, LANES), *surf_parts)
+    )(recv.reshape(owners * ROWS, LANES), active.reshape(1, LANES), *surf_parts)
     ends = exchange(ends.reshape(owners, 24, LANES), "col")
     for k, mask in enumerate(doublings(groups)):
         if k:

time: 105 us -> 104 us (level)
  no operation moved by 1% of the time
where the time goes in v4:
time: 104 us; the launch traced here: 103 us
  starting transfers between devices  60.8 us (58%)
  waiting for transfers between devices  25.9 us (25%)
  Pallas kernels  15.4 us (15%)
    ppermute x8, starting transfers between devices, swap(): return lax.ppermute(x, 'grp', [(i, i ^ mask) for i in range(n)])  32.3 us
    all_to_all x3, starting transfers between devices, exchange(): return lax.all_to_all(x, axis, split_axis=0, concat_axis=0, tiled=True)  28.5 us
    ppermute x8, waiting for transfers between devices, swap(): return lax.ppermute(x, 'grp', [(i, i ^ mask) for i in range(n)])  17.2 us
    all_to_all x3, waiting for transfers between devices, exchange(): return lax.all_to_all(x, axis, split_axis=0, concat_axis=0, tiled=True)  8.68 us
    pallas_call x1, Pallas kernels, step(): pl.pallas_call(speciate_kernel, out_shape=sds((comps, depth, width), F32)...  5.6 us
    pallas_call x1, Pallas kernels, step(): pl.pallas_call(eliminate_kernel, out_shape=(held((owners * ROWS, LANES)),...  4.83 us
  transfers between devices with their start and end apart: 11, of which 8 were waited for; matrix products, arithmetic and copies ran while one was open for 0% of the time, Pallas kernels for 2%

profile of v4, /device:TPU:2, one launch (start us, length us, event | category | flops | bytes accessed | tf_op | source)
XLA Modules:
  0.0 103.3 jit_solution(227308285347180081)
XLA Ops:
  0.6 1.3 %meta.1 = s32[32,2,128]{2,1,0:T(2,128)} custom-call(s32[1,128]{1,0:T(1,128)} %bitcast.22, s32[1,128]{1,0:T(1,128)} %bitcast.19), custom_call_target="tpu_custom_call" | custom-call | tf_op jit(solution)/shard_map/meta/pallas_call | solution.py:444
  1.9 13.5 %all-to-all-start = ((s32[32,2,128]{2,1,0:T(2,128)}), s32[32,2,128]{2,1,0:T(2,128)S(1)}, u32[]{:S(2)}, u32[]{:S(2)}) async-start(s32[32,2,128]{2,1,0:T(2,128)} %meta.1), calls=%async_computation | async-start | bytes 65536 | tf_op jit(solution)/shard_map/all_to_all | solution.py:420
  15.4 8.7 %all-to-all-done.meta_ref = s32[32,2,128]{2,1,0:T(2,128)S(1)} async-done(((s32[32,2,128]{2,1,0:T(2,128)}), s32[32,2,128]{2,1,0:T(2,128)S(1)}, u32[]{:S(2)}, u32[]{:S(2)}) %all-to-all-start) | async-done | bytes 32800 | tf_op jit(solution)/shard_map/all_to_all | solution.py:420
  24.1 4.8 %eliminate.1 = (f32[928,128]{1,0:T(8,128)}, f32[12,8,4096]{2,1,0:T(8,128)S(1)}, f32[2,8,4096]{2,1,0:T(8,128)S(1)}) custom-call(s32[1]{0:T(128)} %bitcast.first_ref, f32[16]{0:T(128)} %table_ref.1, f32[12,8,4096]{2,1,0:T(8,128)} %conc_hbm.1, f32[8,4096]{1,0:T(8,128)} %theta_ref.1, f32[8,4096]{1,0:T(8,128)} %cond_hbm.1, s32[32,2,128]{2,1,0:T(2,128)S(1)} %all-to-all-done.meta_ref), custom_call_target="tpu_custom_call" | custom-call | tf_op jit(solution)/shard_map/eliminate/pallas_call | solution.py:481
  29.0 5.2 %all-to-all-start.1 = ((f32[32,29,1,128]{3,2,1,0:T(1,128)}), f32[32,29,1,128]{3,2,1,0:T(1,128)S(1)}, u32[]{:S(2)}, u32[]{:S(2)}) async-start(f32[32,29,1,128]{3,2,1,0:T(1,128)} %bitcast.3), calls=%async_computation.1 | async-start | bytes 950272 | tf_op jit(solution)/shard_map/all_to_all | solution.py:420
  34.2 1.1 %surf_pack.1 = (f32[8,16,128]{2,1,0:T(8,128)S(1)}, f32[8,16,128]{2,1,0:T(8,128)S(1)}) custom-call(s32[1]{0:T(128)} %bitcast.5.me_ref, f32[12,512]{1,0:T(8,128)} %conc_ref.3, f32[1,512]{1,0:T(1,128)} %bitcast.13, s32[1,512]{1,0:T(1,128)} %bitcast.15, s32[1,512]{1,0:T(1,128)} %bitcast.17), custom_call_target="tpu_custom_call" | custom-call | tf_op jit(solution)/shard_map/surf_pack/pallas_call | solution.py:461
  35.4 7.7 %collective-permute-start = (f32[8,16,128]{2,1,0:T(8,128)S(1)}, f32[8,16,128]{2,1,0:T(8,128)S(1)}, u32[]{:S(2)}, u32[]{:S(2)}) collective-permute-start(f32[8,16,128]{2,1,0:T(8,128)S(1)} %get-tuple-element.13), channel_id=1, source_target_pairs={{0,256},{32,288},{64,320},{96,352},{128,384},{160,416},{192,448},{... | collective-permute-start | bytes 196616 | tf_op jit(solution)/shard_map/ppermute | solution.py:401
  43.1 2.5 %collective-permute-done = f32[8,16,128]{2,1,0:T(8,128)S(1)} collective-permute-done((f32[8,16,128]{2,1,0:T(8,128)S(1)}, f32[8,16,128]{2,1,0:T(8,128)S(1)}, u32[]{:S(2)}, u32[]{:S(2)}) %collective-permute-start) | collective-permute-done | bytes 65568 | tf_op jit(solution)/shard_map/ppermute | solution.py:401
  45.6 4.9 %collective-permute-start.1 = (f32[4,16,128]{2,1,0:T(8,128)S(1)}, f32[4,16,128]{2,1,0:T(8,128)S(1)}, u32[]{:S(2)}, u32[]{:S(2)}) collective-permute-start(f32[4,16,128]{2,1,0:T(8,128)S(1)} %slice_add_fusion), channel_id=1, source_target_pairs={{0,128},{32,160},{64,192},{96,224},{128,0},{160,32},{192,64},{224,... | collective-permute-start | bytes 98312 | tf_op jit(solution)/shard_map/ppermute | solution.py:401
  50.5 1.9 %collective-permute-done.1 = f32[4,16,128]{2,1,0:T(8,128)S(1)} collective-permute-done((f32[4,16,128]{2,1,0:T(8,128)S(1)}, f32[4,16,128]{2,1,0:T(8,128)S(1)}, u32[]{:S(2)}, u32[]{:S(2)}) %collective-permute-start.1) | collective-permute-done | bytes 32800 | tf_op jit(solution)/shard_map/ppermute | solution.py:401
  52.4 3.3 %collective-permute-start.2 = (f32[2,16,128]{2,1,0:T(8,128)S(1)}, f32[2,16,128]{2,1,0:T(8,128)S(1)}, u32[]{:S(2)}, u32[]{:S(2)}) collective-permute-start(f32[2,16,128]{2,1,0:T(8,128)S(1)} %slice_add_fusion.1), channel_id=1, source_target_pairs={{0,64},{32,96},{64,0},{96,32},{128,192},{160,224},{192,128},{224,1... | collective-permute-start | bytes 49160 | tf_op jit(solution)/shard_map/ppermute | solution.py:401
  55.7 2.3 %collective-permute-done.2 = f32[2,16,128]{2,1,0:T(8,128)S(1)} collective-permute-done((f32[2,16,128]{2,1,0:T(8,128)S(1)}, f32[2,16,128]{2,1,0:T(8,128)S(1)}, u32[]{:S(2)}, u32[]{:S(2)}) %collective-permute-start.2) | collective-permute-done | bytes 16416 | tf_op jit(solution)/shard_map/ppermute | solution.py:401
  58.0 1.9 %collective-permute-start.3 = (f32[1,16,128]{2,1,0:T(8,128)S(1)}, f32[1,16,128]{2,1,0:T(8,128)S(1)}, u32[]{:S(2)}, u32[]{:S(2)}) collective-permute-start(f32[1,16,128]{2,1,0:T(8,128)S(1)} %get-tuple-element.16), channel_id=1, source_target_pairs={{0,32},{32,0},{64,96},{96,64},{128,160},{160,128},{192,224},{224,1... | collective-permute-start | bytes 24584 | tf_op jit(solution)/shard_map/ppermute | solution.py:401
  61.1 1.2 %interface.1 = (f32[768,128]{1,0:T(8,128)}, f32[1,16,128]{2,1,0:T(8,128)S(1)}) custom-call(f32[928,128]{1,0:T(8,128)S(1)} %bitcast.12, s32[1,128]{1,0:T(1,128)S(1)} %bitcast.20, f32[1,16,128]{2,1,0:T(8,128)S(1)} %get-tuple-element.17.refs_0_, f32[1,16,128]{2,1,0:T(8,128)S(1)} %get-tuple-element.18.refs_1_, f32[1,16,128]{2,1,0:T(8,128)S(1)} %get-tuple-element.19.refs_2_, ...), custom_call_target="tpu_custom_call" | custom-call | tf_op jit(solution)/shard_map/interface/pallas_call | solution.py:416
  62.3 8.3 %collective-permute-start.4 = (f32[1,16,128]{2,1,0:T(8,128)S(1)}, f32[1,16,128]{2,1,0:T(8,128)S(1)}, u32[]{:S(2)}, u32[]{:S(2)}) collective-permute-start(f32[1,16,128]{2,1,0:T(8,128)S(1)} %get-tuple-element.15), channel_id=1, source_target_pairs={{0,256},{32,288},{64,320},{96,352},{128,384},{160,416},{192,448},{... | collective-permute-start | bytes 24584 | tf_op jit(solution)/shard_map/ppermute | solution.py:401
  70.5 9.9 %all-to-all-start.2 = ((f32[32,24,128]{2,1,0:T(8,128)}), f32[32,24,128]{2,1,0:T(8,128)S(1)}, u32[]{:S(2)}, u32[]{:S(2)}) async-start(f32[32,24,128]{2,1,0:T(8,128)} %bitcast.9), calls=%async_computation.2 | async-start | bytes 786432 | tf_op jit(solution)/shard_map/all_to_all | solution.py:420
  80.4 1.9 %collective-permute-start.5 = (f32[2,16,128]{2,1,0:T(8,128)S(1)}, f32[2,16,128]{2,1,0:T(8,128)S(1)}, u32[]{:S(2)}, u32[]{:S(2)}) collective-permute-start(f32[2,16,128]{2,1,0:T(8,128)S(1)} %pad_maximum_fusion.1), channel_id=1, source_target_pairs={{0,32},{32,0},{64,96},{96,64},{128,160},{160,128},{192,224},{224,1... | collective-permute-start | bytes 49160 | tf_op jit(solution)/shard_map/ppermute | solution.py:401
  82.4 1.1 %collective-permute-done.5 = f32[2,16,128]{2,1,0:T(8,128)S(1)} collective-permute-done((f32[2,16,128]{2,1,0:T(8,128)S(1)}, f32[2,16,128]{2,1,0:T(8,128)S(1)}, u32[]{:S(2)}, u32[]{:S(2)}) %collective-permute-start.5) | collective-permute-done | bytes 16416 | tf_op jit(solution)/shard_map/ppermute | solution.py:401
  83.5 2.1 %collective-permute-start.6 = (f32[4,16,128]{2,1,0:T(8,128)S(1)}, f32[4,16,128]{2,1,0:T(8,128)S(1)}, u32[]{:S(2)}, u32[]{:S(2)}) collective-permute-start(f32[4,16,128]{2,1,0:T(8,128)S(1)} %pad_maximum_fusion), channel_id=1, source_target_pairs={{0,64},{32,96},{64,0},{96,32},{128,192},{160,224},{192,128},{224,1... | collective-permute-start | bytes 98312 | tf_op jit(solution)/shard_map/ppermute | solution.py:401
  85.6 3.7 %collective-permute-done.6 = f32[4,16,128]{2,1,0:T(8,128)S(1)} collective-permute-done((f32[4,16,128]{2,1,0:T(8,128)S(1)}, f32[4,16,128]{2,1,0:T(8,128)S(1)}, u32[]{:S(2)}, u32[]{:S(2)}) %collective-permute-start.6) | collective-permute-done | bytes 32800 | tf_op jit(solution)/shard_map/ppermute | solution.py:401
  89.3 2.1 %collective-permute-start.7 = (f32[8,16,128]{2,1,0:T(8,128)S(1)}, f32[8,16,128]{2,1,0:T(8,128)S(1)}, u32[]{:S(2)}, u32[]{:S(2)}) collective-permute-start(f32[8,16,128]{2,1,0:T(8,128)S(1)} %constant_dynamic-update-slice_fusion.near_ref), channel_id=1, source_target_pairs={{0,128},{32,160},{64,192},{96,224},{128,0},{160,32},{192,64},{224,... | collective-permute-start | bytes 196616 | tf_op jit(solution)/shard_map/ppermute | solution.py:401
  91.9 4.8 %collective-permute-done.7.far_ref = f32[8,16,128]{2,1,0:T(8,128)S(1)} collective-permute-done((f32[8,16,128]{2,1,0:T(8,128)S(1)}, f32[8,16,128]{2,1,0:T(8,128)S(1)}, u32[]{:S(2)}, u32[]{:S(2)}) %collective-permute-start.7) | collective-permute-done | bytes 65568 | tf_op jit(solution)/shard_map/ppermute | solution.py:401
  96.7 1.0 surf_flux.1
  97.7 5.6 %speciate.1 = f32[12,8,4096]{2,1,0:T(8,128)} custom-call(f32[12,8,4096]{2,1,0:T(8,128)S(1)} %get-tuple-element.9.g_ref, f32[2,8,4096]{2,1,0:T(8,128)S(1)} %get-tuple-element.10.vw_ref, f32[8,4096]{1,0:T(8,128)S(1)} %copy-done, f32[32,24,128]{2,1,0:T(8,128)S(1)} %all-to-all-done.2.ends_ref, f32[32,16,128]{2,1,0:T(8,128)S(1)} %lookup.1.sorb_ref), custom_call_target="tpu_custom_call" | custom-call | tf_op jit(solution)/shard_map/speciate/pallas_call | solution.py:519
  (34 shorter events, 1.7 us)
Async XLA Ops:
  1.9 22.1 %all-to-all-start = ((s32[32,2,128]{2,1,0:T(2,128)}), s32[32,2,128]{2,1,0:T(2,128)S(1)}, u32[]{:S(2)}, u32[]{:S(2)}) async-start(s32[32,2,128]{2,1,0:T(2,128)} %meta.1), calls=%async_computation | async-start | bytes 65536 | tf_op jit(solution)/shard_map/all_to_all | solution.py:420
  24.1 35.9 %copy-start.6 = (f32[16,12]{1,0:T(8,128)S(1)}, f32[16,12]{1,0:T(8,128)}, u32[]{:S(2)}) copy-start(f32[16,12]{1,0:T(8,128)} %param.18) | copy-start | bytes 2308
  24.1 37.0 %copy-start.5 = (s32[128]{0:T(128)S(1)}, s32[128]{0:T(128)}, u32[]{:S(2)}) copy-start(s32[128]{0:T(128)} %param.16) | copy-start | bytes 1540
  28.9 62.5 %copy-start.7 = (f32[16]{0:T(128)S(1)}, f32[16]{0:T(128)}, u32[]{:S(2)}) copy-start(f32[16]{0:T(128)} %param.19) | copy-start | bytes 196
  28.9 67.8 %copy-start.1 = (f32[12,512]{1,0:T(8,128)S(1)}, f32[12,512]{1,0:T(8,128)}, u32[]{:S(2)}) copy-start(f32[12,512]{1,0:T(8,128)} %conc_ref.3) | copy-start | bytes 73732
  28.9 67.8 %copy-start.2 = (f32[512]{0:T(512)S(1)}, f32[512]{0:T(512)}, u32[]{:S(2)}) copy-start(f32[512]{0:T(512)} %param.21) | copy-start | bytes 6148
  29.0 67.8 %copy-start.3 = (s32[512,1]{0,1:T(1,128)S(1)}, s32[512,1]{0,1:T(1,128)}, u32[]{:S(2)}) copy-start(s32[512,1]{0,1:T(1,128)} %param.22) | copy-start | bytes 6148
  29.0 67.8 %copy-start.4 = (s32[512]{0:T(512)S(1)}, s32[512]{0:T(512)}, u32[]{:S(2)}) copy-start(s32[512]{0:T(512)} %param.23) | copy-start | bytes 6148
  29.0 68.7 %copy-start = (f32[8,4096]{1,0:T(8,128)S(1)}, f32[8,4096]{1,0:T(8,128)}, u32[]{:S(2)}) copy-start(f32[8,4096]{1,0:T(8,128)} %theta_ref.1) | copy-start | bytes 393220
  29.0 32.1 %all-to-all-start.1 = ((f32[32,29,1,128]{3,2,1,0:T(1,128)}), f32[32,29,1,128]{3,2,1,0:T(1,128)S(1)}, u32[]{:S(2)}, u32[]{:S(2)}) async-start(f32[32,29,1,128]{3,2,1,0:T(1,128)} %bitcast.3), calls=%async_computation.1 | async-start | bytes 950272 | tf_op jit(solution)/shard_map/all_to_all | solution.py:420
  35.4 10.2 %collective-permute-start = (f32[8,16,128]{2,1,0:T(8,128)S(1)}, f32[8,16,128]{2,1,0:T(8,128)S(1)}, u32[]{:S(2)}, u32[]{:S(2)}) collective-permute-start(f32[8,16,128]{2,1,0:T(8,128)S(1)} %get-tuple-element.13), channel_id=1, source_target_pairs={{0,256},{32,288},{64,320},{96,352},{128,384},{160,416},{192,448},{... | collective-permute-start | bytes 196616 | tf_op jit(solution)/shard_map/ppermute | solution.py:401
  45.6 6.8 %collective-permute-start.1 = (f32[4,16,128]{2,1,0:T(8,128)S(1)}, f32[4,16,128]{2,1,0:T(8,128)S(1)}, u32[]{:S(2)}, u32[]{:S(2)}) collective-permute-start(f32[4,16,128]{2,1,0:T(8,128)S(1)} %slice_add_fusion), channel_id=1, source_target_pairs={{0,128},{32,160},{64,192},{96,224},{128,0},{160,32},{192,64},{224,... | collective-permute-start | bytes 98312 | tf_op jit(solution)/shard_map/ppermute | solution.py:401
  52.4 5.6 %collective-permute-start.2 = (f32[2,16,128]{2,1,0:T(8,128)S(1)}, f32[2,16,128]{2,1,0:T(8,128)S(1)}, u32[]{:S(2)}, u32[]{:S(2)}) collective-permute-start(f32[2,16,128]{2,1,0:T(8,128)S(1)} %slice_add_fusion.1), channel_id=1, source_target_pairs={{0,64},{32,96},{64,0},{96,32},{128,192},{160,224},{192,128},{224,1... | collective-permute-start | bytes 49160 | tf_op jit(solution)/shard_map/ppermute | solution.py:401
  58.0 3.1 %collective-permute-start.3 = (f32[1,16,128]{2,1,0:T(8,128)S(1)}, f32[1,16,128]{2,1,0:T(8,128)S(1)}, u32[]{:S(2)}, u32[]{:S(2)}) collective-permute-start(f32[1,16,128]{2,1,0:T(8,128)S(1)} %get-tuple-element.16), channel_id=1, source_target_pairs={{0,32},{32,0},{64,96},{96,64},{128,160},{160,128},{192,224},{224,1... | collective-permute-start | bytes 24584 | tf_op jit(solution)/shard_map/ppermute | solution.py:401
  62.3 18.1 %collective-permute-start.4 = (f32[1,16,128]{2,1,0:T(8,128)S(1)}, f32[1,16,128]{2,1,0:T(8,128)S(1)}, u32[]{:S(2)}, u32[]{:S(2)}) collective-permute-start(f32[1,16,128]{2,1,0:T(8,128)S(1)} %get-tuple-element.15), channel_id=1, source_target_pairs={{0,256},{32,288},{64,320},{96,352},{128,384},{160,416},{192,448},{... | collective-permute-start | bytes 24584 | tf_op jit(solution)/shard_map/ppermute | solution.py:401
  70.5 27.2 %all-to-all-start.2 = ((f32[32,24,128]{2,1,0:T(8,128)}), f32[32,24,128]{2,1,0:T(8,128)S(1)}, u32[]{:S(2)}, u32[]{:S(2)}) async-start(f32[32,24,128]{2,1,0:T(8,128)} %bitcast.9), calls=%async_computation.2 | async-start | bytes 786432 | tf_op jit(solution)/shard_map/all_to_all | solution.py:420
  80.4 3.1 %collective-permute-start.5 = (f32[2,16,128]{2,1,0:T(8,128)S(1)}, f32[2,16,128]{2,1,0:T(8,128)S(1)}, u32[]{:S(2)}, u32[]{:S(2)}) collective-permute-start(f32[2,16,128]{2,1,0:T(8,128)S(1)} %pad_maximum_fusion.1), channel_id=1, source_target_pairs={{0,32},{32,0},{64,96},{96,64},{128,160},{160,128},{192,224},{224,1... | collective-permute-start | bytes 49160 | tf_op jit(solution)/shard_map/ppermute | solution.py:401
  83.5 5.8 %collective-permute-start.6 = (f32[4,16,128]{2,1,0:T(8,128)S(1)}, f32[4,16,128]{2,1,0:T(8,128)S(1)}, u32[]{:S(2)}, u32[]{:S(2)}) collective-permute-start(f32[4,16,128]{2,1,0:T(8,128)S(1)} %pad_maximum_fusion), channel_id=1, source_target_pairs={{0,64},{32,96},{64,0},{96,32},{128,192},{160,224},{192,128},{224,1... | collective-permute-start | bytes 98312 | tf_op jit(solution)/shard_map/ppermute | solution.py:401
  89.3 7.4 %collective-permute-start.7 = (f32[8,16,128]{2,1,0:T(8,128)S(1)}, f32[8,16,128]{2,1,0:T(8,128)S(1)}, u32[]{:S(2)}, u32[]{:S(2)}) collective-permute-start(f32[8,16,128]{2,1,0:T(8,128)S(1)} %constant_dynamic-update-slice_fusion.near_ref), channel_id=1, source_target_pairs={{0,128},{32,160},{64,192},{96,224},{128,0},{160,32},{192,64},{224,... | collective-permute-start | bytes 196616 | tf_op jit(solution)/shard_map/ppermute | solution.py:401

commit v5 on v4

--- a/solution.py
+++ b/solution.py
@@ -30,8 +30,15 @@
 
 
 def surf_pack_kernel(
-    me_ref, conc_ref, rate_ref, group_ref, local_ref, keep_ref, send_ref, lhs_ref
+    me_ref, conc_ref, rate_ref, group_ref, local_ref, *refs
 ):
+    brick_hbm, refs = refs[:3], refs[3:]
+    keep_ref, send_ref, *brick, lhs_ref, sems = refs
+    copies = [
+        pltpu.make_async_copy(brick_hbm[k], brick[k], sems.at[k]) for k in range(3)
+    ]
+    for copy in copies:
+        copy.start()
     comps, n = conc_ref.shape
     half = send_ref.shape[0]
     rate = rate_ref[...]
@@ -41,7 +48,7 @@
     parts = [part.astype(F32) for part in split3(vals)]
     slot = group_ref[...] ^ me_ref[0]
     for b in range(2 * half):
-        keep = slot == b
+        keep = slot == half_mask(b, 2 * half)
         for i, part in enumerate(parts):
             lhs_ref[i, 16 * b : 16 * b + 16, :] = jnp.where(keep, part, 0.0).astype(
                 jnp.bfloat16
@@ -55,6 +62,8 @@
     total = total.reshape(2 * half, 16, LANES)
     keep_ref[...] = total[:half]
     send_ref[...] = total[half:]
+    for copy in copies:
+        copy.wait()
 
 
 def surf_flux_kernel(
@@ -84,6 +93,15 @@
     return masks
 
 
+def partners(n):
+    masks = halvings(n)
+    return [masks[k] for k in (3, 0, 2, 1) if k < len(masks)]
+
+
+def half_mask(b, n):
+    return sum(p for m, p in zip(halvings(n), partners(n)) if b & m)
+
+
 def doublings(n):
     masks = halvings(n)
     return [masks[k] for k in (0, 3, 2, 1) if k < len(masks)]
@@ -96,38 +114,15 @@
 def eliminate_kernel(
     first_ref,
     table_ref,
-    conc_hbm,
-    theta_hbm,
-    cond_hbm,
+    conc_ref,
+    theta_ref,
+    cond_ref,
     meta_ref,
     send_ref,
     g_ref,
     vw_ref,
-    conc_ref,
-    theta_ref,
-    cond_ref,
-    sems,
 ):
     comps = conc_ref.shape[0]
-    wide = conc_ref.shape[2] // CHUNKS
-
-    def in_copies(n):
-        part = pl.ds(pl.multiple_of(n * wide, wide), wide)
-        return [
-            pltpu.make_async_copy(
-                theta_hbm.at[:, part], theta_ref.at[:, part], sems.at[3 * n]
-            ),
-            pltpu.make_async_copy(
-                cond_hbm.at[:, part], cond_ref.at[:, part], sems.at[3 * n + 1]
-            ),
-            pltpu.make_async_copy(
-                conc_hbm.at[:, :, part], conc_ref.at[:, :, part], sems.at[3 * n + 2]
-            ),
-        ]
-
-    for n in range(CHUNKS):
-        for copy in in_copies(n):
-            copy.start()
     tiles = send_ref.shape[0] // ROWS
     shape = (8, LANES)
     row = rows_iota(shape)
@@ -137,7 +132,11 @@
     def roll(v, d):
         return pltpu.roll(v, d % 8, 0)
 
-    def tile(t):
+    def read(t):
+        cols = pl.ds(pl.multiple_of(t * LANES, LANES), LANES)
+        return [conc_ref[j, :, cols] for j in range(comps)]
+
+    def tile(t, conc):
         cols = pl.ds(pl.multiple_of(t * LANES, LANES), LANES)
         classes = meta_ref[t, 0:1, :]
         active = meta_ref[t, 1:2, :]
@@ -193,26 +192,24 @@
         put(26, w, 0)
         put(27, scaled, 0)
         put(28, scaled, 7)
+        found = []
         for j in range(comps):
-            x = solve(theta * conc_ref[j, :, cols])
-            g_ref[j, :, cols] = jnp.where(inner, x, zero)
+            x = solve(theta * conc[j])
+            found.append(jnp.where(inner, x, zero))
             put(j, x, 0)
             put(12 + j, x, 7)
+        return cols, found
 
     def tiles_of(i, carry):
-        for k in range(FEW):
-            tile(i * FEW + k)
+        group = [i * FEW + k for k in range(FEW)]
+        conc = [read(t) for t in group]
+        done = [tile(t, c) for t, c in zip(group, conc)]
+        for cols, found in done:
+            for j in range(comps):
+                g_ref[j, :, cols] = found[j]
         return carry
 
-    per = tiles // FEW // CHUNKS
-
-    def chunk(n, carry):
-        for copy in in_copies(n):
-            copy.wait()
-        lax.fori_loop(n * per, (n + 1) * per, tiles_of, 0)
-        return carry
-
-    lax.fori_loop(0, CHUNKS, chunk, 0)
+    lax.fori_loop(0, tiles // FEW, tiles_of, 0)
 
 
 FEW = 4
@@ -458,24 +455,34 @@
     smem = pl.BlockSpec(memory_space=pltpu.SMEM)
     me = lax.axis_index("grp").astype(jnp.int32).reshape(1)
     masks = halvings(groups)
-    keep, surf_send = pl.pallas_call(
+    keep, surf_send, *brick = pl.pallas_call(
         surf_pack_kernel,
         out_shape=(
             sds((groups // 2, 16, LANES), F32),
             sds((groups // 2, 16, LANES), F32),
+            held((comps, depth, width)),
+            held((depth, width)),
+            held((depth, width)),
         ),
-        in_specs=[smem] + [full()] * 4,
-        out_specs=(full(), full()),
-        scratch_shapes=[pltpu.VMEM((3, 16 * groups, n), jnp.bfloat16)],
+        in_specs=[smem] + [full()] * 4 + [pl.BlockSpec(memory_space=HBM)] * 3,
+        out_specs=tuple(full() for _ in range(5)),
+        scratch_shapes=[
+            pltpu.VMEM((3, 16 * groups, n), jnp.bfloat16),
+            pltpu.SemaphoreType.DMA((3,)),
+        ],
         interpret=INTERPRET,
         compiler_params=pltpu.CompilerParams(vmem_limit_bytes=24 << 20),
         name="surf_pack",
-    )(me, *(far(x) for x in (surf_conc, rate, group, local)))
+    )(
+        me,
+        *(far(x) for x in (surf_conc, rate, group, local)),
+        *(far(x) for x in (conc, porosity, cell_cond)),
+    )
     surf_parts = [keep]
-    for k, mask in enumerate(masks):
+    for k, (mask, partner) in enumerate(zip(masks, partners(groups))):
         if k:
             surf_send = sum(x[mask : 2 * mask] for x in surf_parts)
-        surf_parts.append(swap(surf_send, mask))
+        surf_parts.append(swap(surf_send, partner))
     surf_parts = [x[:1] for x in surf_parts]
 
     send, g, vw = pl.pallas_call(
@@ -485,18 +492,13 @@
             held((comps, depth, width)),
             held((2, depth, width)),
         ),
-        in_specs=[smem, smem] + [pl.BlockSpec(memory_space=HBM)] * 3 + [full()],
+        in_specs=[smem, smem] + [full()] * 4,
         out_specs=(full(), full(), full()),
-        scratch_shapes=[
-            pltpu.VMEM((comps, depth, width), F32),
-            pltpu.VMEM((depth, width), F32),
-            pltpu.VMEM((depth, width), F32),
-            pltpu.SemaphoreType.DMA((3 * CHUNKS,)),
-        ],
         interpret=INTERPRET,
         compiler_params=pltpu.CompilerParams(vmem_limit_bytes=24 << 20),
+        input_output_aliases={2: 1},
         name="eliminate",
-    )(first, far(class_cond), far(conc), far(porosity), far(cell_cond), near(meta))
+    )(first, far(class_cond), *(near(x) for x in brick), near(meta))
     recv = exchange(send.reshape(owners, ROWS, 1, LANES), "col")
 
     table = jnp.concatenate(

time: 104 us -> 101 us (0.971)
  waiting for transfers between devices: 25.9 us -> 22.6 us
    all_to_all x3, waiting for transfers between devices: 8.68 us -> 6.42 us  [exchange(): return lax.all_to_all(x, axis, split_axis=0, concat_axis=0, tiled=True)]
    pallas_call x1, Pallas kernels: 4.83 us -> 3.42 us  [step(): pl.pallas_call(eliminate_kernel, out_shape=(held((owners * ROWS, LANES)),...]
    pallas_call x1, Pallas kernels: 1.15 us -> 2.23 us  [step(): pl.pallas_call(surf_pack_kernel, out_shape=(sds((groups // 2, 16, LANES),...]
  transfers between devices with their start and end apart: 11 -> 11, of which waited for: 8 -> 8; matrix products, arithmetic and copies ran while one was open for 0% -> 0% of each run, Pallas kernels for 2% -> 4%
where the time goes in v5:
time: 101 us; the launch traced here: 100 us
  starting transfers between devices  61.2 us (61%)
  waiting for transfers between devices  22.6 us (22%)
  Pallas kernels  15.1 us (15%)
    ppermute x8, starting transfers between devices, swap(): return lax.ppermute(x, 'grp', [(i, i ^ mask) for i in range(n)])  32.7 us
    all_to_all x3, starting transfers between devices, exchange(): return lax.all_to_all(x, axis, split_axis=0, concat_axis=0, tiled=True)  28.5 us
    ppermute x8, waiting for transfers between devices, swap(): return lax.ppermute(x, 'grp', [(i, i ^ mask) for i in range(n)])  16.2 us
    all_to_all x3, waiting for transfers between devices, exchange(): return lax.all_to_all(x, axis, split_axis=0, concat_axis=0, tiled=True)  6.42 us
    pallas_call x1, Pallas kernels, step(): pl.pallas_call(speciate_kernel, out_shape=sds((comps, depth, width), F32)...  5.6 us
    pallas_call x1, Pallas kernels, step(): pl.pallas_call(eliminate_kernel, out_shape=(held((owners * ROWS, LANES)),...  3.42 us
    pallas_call x1, Pallas kernels, step(): pl.pallas_call(surf_pack_kernel, out_shape=(sds((groups // 2, 16, LANES),...  2.23 us
  transfers between devices with their start and end apart: 11, of which 8 were waited for; matrix products, arithmetic and copies ran while one was open for 0% of the time, Pallas kernels for 4%

profile of v5, /device:TPU:2, one launch (start us, length us, event | category | flops | bytes accessed | tf_op | source)
XLA Modules:
  0.0 100.1 jit_solution(8348620814932704998)
XLA Ops:
  0.6 1.3 %meta.1 = s32[32,2,128]{2,1,0:T(2,128)} custom-call(s32[1,128]{1,0:T(1,128)} %bitcast.22, s32[1,128]{1,0:T(1,128)} %bitcast.19), custom_call_target="tpu_custom_call" | custom-call | tf_op jit(solution)/shard_map/meta/pallas_call | solution.py:441
  1.9 13.5 %all-to-all-start = ((s32[32,2,128]{2,1,0:T(2,128)}), s32[32,2,128]{2,1,0:T(2,128)S(1)}, u32[]{:S(2)}, u32[]{:S(2)}) async-start(s32[32,2,128]{2,1,0:T(2,128)} %meta.1), calls=%async_computation | async-start | bytes 65536 | tf_op jit(solution)/shard_map/all_to_all | solution.py:417
  15.4 2.2 %surf_pack.1 = (f32[8,16,128]{2,1,0:T(8,128)S(1)}, f32[8,16,128]{2,1,0:T(8,128)S(1)}, f32[12,8,4096]{2,1,0:T(8,128)S(1)}, f32[8,4096]{1,0:T(8,128)S(1)}, f32[8,4096]{1,0:T(8,128)S(1)}) custom-call(s32[1]{0:T(128)} %bitcast.1.me_ref, f32[12,512]{1,0:T(8,128)} %conc_ref.3, f32[1,512]{1,0:T(1,128)} %bitcast.13, s32[1,512]{1,0:T(1,128)} %bitcast.15, ...), custom_call_target="tpu_custom_call" | custom-call | tf_op jit(solution)/shard_map/surf_pack/pallas_call | solution.py:458
  17.7 6.4 %all-to-all-done.meta_ref = s32[32,2,128]{2,1,0:T(2,128)S(1)} async-done(((s32[32,2,128]{2,1,0:T(2,128)}), s32[32,2,128]{2,1,0:T(2,128)S(1)}, u32[]{:S(2)}, u32[]{:S(2)}) %all-to-all-start) | async-done | bytes 32800 | tf_op jit(solution)/shard_map/all_to_all | solution.py:417
  24.1 3.4 %eliminate.1 = (f32[928,128]{1,0:T(8,128)}, f32[12,8,4096]{2,1,0:T(8,128)S(1)}, f32[2,8,4096]{2,1,0:T(8,128)S(1)}) custom-call(s32[1]{0:T(128)} %bitcast.first_ref, f32[16]{0:T(128)} %table_ref.1, f32[12,8,4096]{2,1,0:T(8,128)S(1)} %get-tuple-element.12.conc_ref, f32[8,4096]{1,0:T(8,128)S(1)} %get-tuple-element.13.theta_ref, ...), custom_call_target="tpu_custom_call", output_to_operand_aliasing={{1}: (2, {})} | custom-call | tf_op jit(solution)/shard_map/eliminate/pallas_call | solution.py:488
  27.5 5.2 %all-to-all-start.1 = ((f32[32,29,1,128]{3,2,1,0:T(1,128)}), f32[32,29,1,128]{3,2,1,0:T(1,128)S(1)}, u32[]{:S(2)}, u32[]{:S(2)}) async-start(f32[32,29,1,128]{3,2,1,0:T(1,128)} %bitcast.7), calls=%async_computation.1 | async-start | bytes 950272 | tf_op jit(solution)/shard_map/all_to_all | solution.py:417
  32.8 1.9 %collective-permute-start = (f32[8,16,128]{2,1,0:T(8,128)S(1)}, f32[8,16,128]{2,1,0:T(8,128)S(1)}, u32[]{:S(2)}, u32[]{:S(2)}) collective-permute-start(f32[8,16,128]{2,1,0:T(8,128)S(1)} %get-tuple-element.19), channel_id=1, source_target_pairs={{0,32},{32,0},{64,96},{96,64},{128,160},{160,128},{192,224},{224,1... | collective-permute-start | bytes 196616 | tf_op jit(solution)/shard_map/ppermute | solution.py:398
  34.7 1.2 %collective-permute-done = f32[8,16,128]{2,1,0:T(8,128)S(1)} collective-permute-done((f32[8,16,128]{2,1,0:T(8,128)S(1)}, f32[8,16,128]{2,1,0:T(8,128)S(1)}, u32[]{:S(2)}, u32[]{:S(2)}) %collective-permute-start) | collective-permute-done | bytes 65568 | tf_op jit(solution)/shard_map/ppermute | solution.py:398
  35.9 7.7 %collective-permute-start.1 = (f32[4,16,128]{2,1,0:T(8,128)S(1)}, f32[4,16,128]{2,1,0:T(8,128)S(1)}, u32[]{:S(2)}, u32[]{:S(2)}) collective-permute-start(f32[4,16,128]{2,1,0:T(8,128)S(1)} %slice_add_fusion), channel_id=1, source_target_pairs={{0,256},{32,288},{64,320},{96,352},{128,384},{160,416},{192,448},{... | collective-permute-start | bytes 98312 | tf_op jit(solution)/shard_map/ppermute | solution.py:398
  43.6 2.0 %collective-permute-done.1 = f32[4,16,128]{2,1,0:T(8,128)S(1)} collective-permute-done((f32[4,16,128]{2,1,0:T(8,128)S(1)}, f32[4,16,128]{2,1,0:T(8,128)S(1)}, u32[]{:S(2)}, u32[]{:S(2)}) %collective-permute-start.1) | collective-permute-done | bytes 32800 | tf_op jit(solution)/shard_map/ppermute | solution.py:398
  45.6 3.5 %collective-permute-start.2 = (f32[2,16,128]{2,1,0:T(8,128)S(1)}, f32[2,16,128]{2,1,0:T(8,128)S(1)}, u32[]{:S(2)}, u32[]{:S(2)}) collective-permute-start(f32[2,16,128]{2,1,0:T(8,128)S(1)} %slice_add_fusion.1), channel_id=1, source_target_pairs={{0,64},{32,96},{64,0},{96,32},{128,192},{160,224},{192,128},{224,1... | collective-permute-start | bytes 49160 | tf_op jit(solution)/shard_map/ppermute | solution.py:398
  49.1 2.1 %collective-permute-done.2 = f32[2,16,128]{2,1,0:T(8,128)S(1)} collective-permute-done((f32[2,16,128]{2,1,0:T(8,128)S(1)}, f32[2,16,128]{2,1,0:T(8,128)S(1)}, u32[]{:S(2)}, u32[]{:S(2)}) %collective-permute-start.2) | collective-permute-done | bytes 16416 | tf_op jit(solution)/shard_map/ppermute | solution.py:398
  51.2 4.7 %collective-permute-start.3 = (f32[1,16,128]{2,1,0:T(8,128)S(1)}, f32[1,16,128]{2,1,0:T(8,128)S(1)}, u32[]{:S(2)}, u32[]{:S(2)}) collective-permute-start(f32[1,16,128]{2,1,0:T(8,128)S(1)} %get-tuple-element.22), channel_id=1, source_target_pairs={{0,128},{32,160},{64,192},{96,224},{128,0},{160,32},{192,64},{224,... | collective-permute-start | bytes 24584 | tf_op jit(solution)/shard_map/ppermute | solution.py:398
  56.1 1.6 %collective-permute-done.3.refs_4_ = f32[1,16,128]{2,1,0:T(8,128)S(1)} collective-permute-done((f32[1,16,128]{2,1,0:T(8,128)S(1)}, f32[1,16,128]{2,1,0:T(8,128)S(1)}, u32[]{:S(2)}, u32[]{:S(2)}) %collective-permute-start.3) | collective-permute-done | bytes 8224 | tf_op jit(solution)/shard_map/ppermute | solution.py:398
  57.7 1.2 %interface.1 = (f32[768,128]{1,0:T(8,128)}, f32[1,16,128]{2,1,0:T(8,128)S(1)}) custom-call(f32[928,128]{1,0:T(8,128)S(1)} %bitcast.12, s32[1,128]{1,0:T(1,128)S(1)} %bitcast.20, f32[1,16,128]{2,1,0:T(8,128)S(1)} %get-tuple-element.23.refs_0_, f32[1,16,128]{2,1,0:T(8,128)S(1)} %get-tuple-element.24.refs_1_, f32[1,16,128]{2,1,0:T(8,128)S(1)} %get-tuple-element.25.refs_2_, ...), custom_call_target="tpu_custom_call" | custom-call | tf_op jit(solution)/shard_map/interface/pallas_call | solution.py:413
  58.9 8.1 %collective-permute-start.4 = (f32[1,16,128]{2,1,0:T(8,128)S(1)}, f32[1,16,128]{2,1,0:T(8,128)S(1)}, u32[]{:S(2)}, u32[]{:S(2)}) collective-permute-start(f32[1,16,128]{2,1,0:T(8,128)S(1)} %get-tuple-element.21), channel_id=1, source_target_pairs={{0,256},{32,288},{64,320},{96,352},{128,384},{160,416},{192,448},{... | collective-permute-start | bytes 24584 | tf_op jit(solution)/shard_map/ppermute | solution.py:398
  66.9 9.9 %all-to-all-start.2 = ((f32[32,24,128]{2,1,0:T(8,128)}), f32[32,24,128]{2,1,0:T(8,128)S(1)}, u32[]{:S(2)}, u32[]{:S(2)}) async-start(f32[32,24,128]{2,1,0:T(8,128)} %bitcast.9), calls=%async_computation.2 | async-start | bytes 786432 | tf_op jit(solution)/shard_map/all_to_all | solution.py:417
  76.8 1.9 %collective-permute-start.5 = (f32[2,16,128]{2,1,0:T(8,128)S(1)}, f32[2,16,128]{2,1,0:T(8,128)S(1)}, u32[]{:S(2)}, u32[]{:S(2)}) collective-permute-start(f32[2,16,128]{2,1,0:T(8,128)S(1)} %pad_maximum_fusion.1), channel_id=1, source_target_pairs={{0,32},{32,0},{64,96},{96,64},{128,160},{160,128},{192,224},{224,1... | collective-permute-start | bytes 49160 | tf_op jit(solution)/shard_map/ppermute | solution.py:398
  78.8 1.1 %collective-permute-done.5 = f32[2,16,128]{2,1,0:T(8,128)S(1)} collective-permute-done((f32[2,16,128]{2,1,0:T(8,128)S(1)}, f32[2,16,128]{2,1,0:T(8,128)S(1)}, u32[]{:S(2)}, u32[]{:S(2)}) %collective-permute-start.5) | collective-permute-done | bytes 16416 | tf_op jit(solution)/shard_map/ppermute | solution.py:398
  79.9 2.5 %collective-permute-start.6 = (f32[4,16,128]{2,1,0:T(8,128)S(1)}, f32[4,16,128]{2,1,0:T(8,128)S(1)}, u32[]{:S(2)}, u32[]{:S(2)}) collective-permute-start(f32[4,16,128]{2,1,0:T(8,128)S(1)} %pad_maximum_fusion), channel_id=1, source_target_pairs={{0,64},{32,96},{64,0},{96,32},{128,192},{160,224},{192,128},{224,1... | collective-permute-start | bytes 98312 | tf_op jit(solution)/shard_map/ppermute | solution.py:398
  82.5 3.2 %collective-permute-done.6 = f32[4,16,128]{2,1,0:T(8,128)S(1)} collective-permute-done((f32[4,16,128]{2,1,0:T(8,128)S(1)}, f32[4,16,128]{2,1,0:T(8,128)S(1)}, u32[]{:S(2)}, u32[]{:S(2)}) %collective-permute-start.6) | collective-permute-done | bytes 32800 | tf_op jit(solution)/shard_map/ppermute | solution.py:398
  85.7 2.4 %collective-permute-start.7 = (f32[8,16,128]{2,1,0:T(8,128)S(1)}, f32[8,16,128]{2,1,0:T(8,128)S(1)}, u32[]{:S(2)}, u32[]{:S(2)}) collective-permute-start(f32[8,16,128]{2,1,0:T(8,128)S(1)} %constant_dynamic-update-slice_fusion.near_ref), channel_id=1, source_target_pairs={{0,128},{32,160},{64,192},{96,224},{128,0},{160,32},{192,64},{224,... | collective-permute-start | bytes 196616 | tf_op jit(solution)/shard_map/ppermute | solution.py:398
  88.6 4.9 %collective-permute-done.7.far_ref = f32[8,16,128]{2,1,0:T(8,128)S(1)} collective-permute-done((f32[8,16,128]{2,1,0:T(8,128)S(1)}, f32[8,16,128]{2,1,0:T(8,128)S(1)}, u32[]{:S(2)}, u32[]{:S(2)}) %collective-permute-start.7) | collective-permute-done | bytes 65568 | tf_op jit(solution)/shard_map/ppermute | solution.py:398
  94.5 5.6 %speciate.1 = f32[12,8,4096]{2,1,0:T(8,128)} custom-call(f32[12,8,4096]{2,1,0:T(8,128)S(1)} %get-tuple-element.15.g_ref, f32[2,8,4096]{2,1,0:T(8,128)S(1)} %get-tuple-element.16.vw_ref, f32[8,4096]{1,0:T(8,128)S(1)} %copy-done, f32[32,24,128]{2,1,0:T(8,128)S(1)} %all-to-all-done.2.ends_ref, f32[32,16,128]{2,1,0:T(8,128)S(1)} %lookup.1.sorb_ref), custom_call_target="tpu_custom_call" | custom-call | tf_op jit(solution)/shard_map/speciate/pallas_call | solution.py:521
  (34 shorter events, 1.7 us)
Async XLA Ops:
  1.9 22.1 %all-to-all-start = ((s32[32,2,128]{2,1,0:T(2,128)}), s32[32,2,128]{2,1,0:T(2,128)S(1)}, u32[]{:S(2)}, u32[]{:S(2)}) async-start(s32[32,2,128]{2,1,0:T(2,128)} %meta.1), calls=%async_computation | async-start | bytes 65536 | tf_op jit(solution)/shard_map/all_to_all | solution.py:417
  17.6 38.3 %copy-start.6 = (f32[16,12]{1,0:T(8,128)S(1)}, f32[16,12]{1,0:T(8,128)}, u32[]{:S(2)}) copy-start(f32[16,12]{1,0:T(8,128)} %param.18) | copy-start | bytes 2308
  17.7 40.0 %copy-start.5 = (s32[128]{0:T(128)S(1)}, s32[128]{0:T(128)}, u32[]{:S(2)}) copy-start(s32[128]{0:T(128)} %param.16) | copy-start | bytes 1540
  27.5 60.6 %copy-start.7 = (f32[16]{0:T(128)S(1)}, f32[16]{0:T(128)}, u32[]{:S(2)}) copy-start(f32[16]{0:T(128)} %param.19) | copy-start | bytes 196
  27.5 66.0 %copy-start.1 = (f32[12,512]{1,0:T(8,128)S(1)}, f32[12,512]{1,0:T(8,128)}, u32[]{:S(2)}) copy-start(f32[12,512]{1,0:T(8,128)} %conc_ref.3) | copy-start | bytes 73732
  27.5 66.0 %copy-start.2 = (f32[512]{0:T(512)S(1)}, f32[512]{0:T(512)}, u32[]{:S(2)}) copy-start(f32[512]{0:T(512)} %param.21) | copy-start | bytes 6148
  27.5 66.0 %copy-start.3 = (s32[512,1]{0,1:T(1,128)S(1)}, s32[512,1]{0,1:T(1,128)}, u32[]{:S(2)}) copy-start(s32[512,1]{0,1:T(1,128)} %param.22) | copy-start | bytes 6148
  27.5 66.0 %copy-start.4 = (s32[512]{0:T(512)S(1)}, s32[512]{0:T(512)}, u32[]{:S(2)}) copy-start(s32[512]{0:T(512)} %param.23) | copy-start | bytes 6148
  27.5 66.9 %copy-start = (f32[8,4096]{1,0:T(8,128)S(1)}, f32[8,4096]{1,0:T(8,128)}, u32[]{:S(2)}) copy-start(f32[8,4096]{1,0:T(8,128)} %theta_ref.1) | copy-start | bytes 393220
  27.5 30.1 %all-to-all-start.1 = ((f32[32,29,1,128]{3,2,1,0:T(1,128)}), f32[32,29,1,128]{3,2,1,0:T(1,128)S(1)}, u32[]{:S(2)}, u32[]{:S(2)}) async-start(f32[32,29,1,128]{3,2,1,0:T(1,128)} %bitcast.7), calls=%async_computation.1 | async-start | bytes 950272 | tf_op jit(solution)/shard_map/all_to_all | solution.py:417
  32.8 3.1 %collective-permute-start = (f32[8,16,128]{2,1,0:T(8,128)S(1)}, f32[8,16,128]{2,1,0:T(8,128)S(1)}, u32[]{:S(2)}, u32[]{:S(2)}) collective-permute-start(f32[8,16,128]{2,1,0:T(8,128)S(1)} %get-tuple-element.19), channel_id=1, source_target_pairs={{0,32},{32,0},{64,96},{96,64},{128,160},{160,128},{192,224},{224,1... | collective-permute-start | bytes 196616 | tf_op jit(solution)/shard_map/ppermute | solution.py:398
  35.9 9.7 %collective-permute-start.1 = (f32[4,16,128]{2,1,0:T(8,128)S(1)}, f32[4,16,128]{2,1,0:T(8,128)S(1)}, u32[]{:S(2)}, u32[]{:S(2)}) collective-permute-start(f32[4,16,128]{2,1,0:T(8,128)S(1)} %slice_add_fusion), channel_id=1, source_target_pairs={{0,256},{32,288},{64,320},{96,352},{128,384},{160,416},{192,448},{... | collective-permute-start | bytes 98312 | tf_op jit(solution)/shard_map/ppermute | solution.py:398
  45.6 5.6 %collective-permute-start.2 = (f32[2,16,128]{2,1,0:T(8,128)S(1)}, f32[2,16,128]{2,1,0:T(8,128)S(1)}, u32[]{:S(2)}, u32[]{:S(2)}) collective-permute-start(f32[2,16,128]{2,1,0:T(8,128)S(1)} %slice_add_fusion.1), channel_id=1, source_target_pairs={{0,64},{32,96},{64,0},{96,32},{128,192},{160,224},{192,128},{224,1... | collective-permute-start | bytes 49160 | tf_op jit(solution)/shard_map/ppermute | solution.py:398
  51.2 6.4 %collective-permute-start.3 = (f32[1,16,128]{2,1,0:T(8,128)S(1)}, f32[1,16,128]{2,1,0:T(8,128)S(1)}, u32[]{:S(2)}, u32[]{:S(2)}) collective-permute-start(f32[1,16,128]{2,1,0:T(8,128)S(1)} %get-tuple-element.22), channel_id=1, source_target_pairs={{0,128},{32,160},{64,192},{96,224},{128,0},{160,32},{192,64},{224,... | collective-permute-start | bytes 24584 | tf_op jit(solution)/shard_map/ppermute | solution.py:398
  58.9 17.9 %collective-permute-start.4 = (f32[1,16,128]{2,1,0:T(8,128)S(1)}, f32[1,16,128]{2,1,0:T(8,128)S(1)}, u32[]{:S(2)}, u32[]{:S(2)}) collective-permute-start(f32[1,16,128]{2,1,0:T(8,128)S(1)} %get-tuple-element.21), channel_id=1, source_target_pairs={{0,256},{32,288},{64,320},{96,352},{128,384},{160,416},{192,448},{... | collective-permute-start | bytes 24584 | tf_op jit(solution)/shard_map/ppermute | solution.py:398
  66.9 27.5 %all-to-all-start.2 = ((f32[32,24,128]{2,1,0:T(8,128)}), f32[32,24,128]{2,1,0:T(8,128)S(1)}, u32[]{:S(2)}, u32[]{:S(2)}) async-start(f32[32,24,128]{2,1,0:T(8,128)} %bitcast.9), calls=%async_computation.2 | async-start | bytes 786432 | tf_op jit(solution)/shard_map/all_to_all | solution.py:417
  76.8 3.1 %collective-permute-start.5 = (f32[2,16,128]{2,1,0:T(8,128)S(1)}, f32[2,16,128]{2,1,0:T(8,128)S(1)}, u32[]{:S(2)}, u32[]{:S(2)}) collective-permute-start(f32[2,16,128]{2,1,0:T(8,128)S(1)} %pad_maximum_fusion.1), channel_id=1, source_target_pairs={{0,32},{32,0},{64,96},{96,64},{128,160},{160,128},{192,224},{224,1... | collective-permute-start | bytes 49160 | tf_op jit(solution)/shard_map/ppermute | solution.py:398
  79.9 5.8 %collective-permute-start.6 = (f32[4,16,128]{2,1,0:T(8,128)S(1)}, f32[4,16,128]{2,1,0:T(8,128)S(1)}, u32[]{:S(2)}, u32[]{:S(2)}) collective-permute-start(f32[4,16,128]{2,1,0:T(8,128)S(1)} %pad_maximum_fusion), channel_id=1, source_target_pairs={{0,64},{32,96},{64,0},{96,32},{128,192},{160,224},{192,128},{224,1... | collective-permute-start | bytes 98312 | tf_op jit(solution)/shard_map/ppermute | solution.py:398
  85.7 7.7 %collective-permute-start.7 = (f32[8,16,128]{2,1,0:T(8,128)S(1)}, f32[8,16,128]{2,1,0:T(8,128)S(1)}, u32[]{:S(2)}, u32[]{:S(2)}) collective-permute-start(f32[8,16,128]{2,1,0:T(8,128)S(1)} %constant_dynamic-update-slice_fusion.near_ref), channel_id=1, source_target_pairs={{0,128},{32,160},{64,192},{96,224},{128,0},{160,32},{192,64},{224,... | collective-permute-start | bytes 196616 | tf_op jit(solution)/shard_map/ppermute | solution.py:398
